TPU v7x, 512 devices: a whole 4x4x16 slice. The times are simulated.
512 devices in a mesh: space: 128 (over z, x_hi, y), depth: 4 (over x_lo, core).
Axes of the slice: x: 4 (x_hi: 2, x_lo: 2; x = x_hi * 2 + x_lo), y: 4, z: 16, core: 2. Of those that a mesh axis runs over, the one named last changes fastest.
Arguments:
- features: bfloat16 [128, 4, 512, 128], P('space', 'depth'), may hold values from -6 to 6
- cotangent: bfloat16 [128, 4, 512, 128], P('space', 'depth'), may hold values from -6 to 6
- first_kernel: bfloat16 [27, 128, 128], replicated, may hold values from -0.109375 to 0.109375
- second_kernel: bfloat16 [27, 128, 128], replicated, may hold values from -0.109375 to 0.109375
- slot_tile: int32 [128, 4], P('space'), may hold values from 0 to 3, as said below
- slot_used: int32 [128, 4], P('space'), may hold values from 0 to 1, as said below
Outputs:
- input_grad: bfloat16 [128, 4, 512, 128], P('space', 'depth')
- first_kernel_grad: float32 [442368], P(('space', 'depth'))
- second_kernel_grad: float32 [442368], P(('space', 'depth'))
Inputs may be any that keep to these rules, and one draw needn't show every extreme that they name: `slot_tile`: in each column the used slots hold distinct z positions that form one unbroken run; in some column every slot is used. `slot_used`: every column has at least one used slot.
All inputs are finite; a program needn't handle non-finite values.
Results may differ from a plain program's by a relative error of at most 0.006.
Values may be sent and summed in bfloat16 or wider, within the bound.
A program may use at most 64 MiB of HBM per device.

v0:
```python
import jax
import jax.numpy as jnp
from jax import lax
from jax.sharding import PartitionSpec as P

TE = 8
GY = 8


SLOPE_COEF = 0.7978845608028654
CUBIC_COEF = 0.044715


def from_behind(block, axis, distance):
    devices = range(lax.axis_size(axis))
    route = [(i - distance, i) for i in devices if i - distance in devices]
    return lax.ppermute(block, axis, route)


def gelu_pair(values):
    inner_arg = SLOPE_COEF * (values + CUBIC_COEF * values * values * values)
    tangent = jnp.tanh(inner_arg)
    output = 0.5 * values * (1.0 + tangent)
    derivative = 0.5 * (1.0 + tangent) + 0.5 * values * (1.0 - tangent * tangent) * SLOPE_COEF * (
        1.0 + 3.0 * CUBIC_COEF * values * values
    )
    return (output, derivative)


def gelu_slope(values):
    inner_arg = SLOPE_COEF * (values + CUBIC_COEF * values * values * values)
    tangent = jnp.tanh(inner_arg)
    return 0.5 * (1.0 + tangent) + 0.5 * values * (1.0 - tangent * tangent) * SLOPE_COEF * (
        1.0 + 3.0 * CUBIC_COEF * values * values
    )


def place_matrix(slot_tile, slot_used, position_count):
    positions = jnp.arange(position_count, dtype=jnp.int32)
    matches = (slot_tile[0][None, :] == positions[:, None]) & (slot_used[0][None, :] == 1)
    return matches.astype(jnp.bfloat16)


def dense_column(tile_rows, placement):
    summed = jnp.einsum(
        "tj,jvc->tvc",
        placement,
        lax.all_gather(tile_rows, "depth", axis=0, tiled=True),
        preferred_element_type=jnp.float32,
    )
    return summed.astype(jnp.bfloat16).reshape(-1, TE, TE, summed.shape[-1])


def extend_sides(own_block, move_face, space_index):
    y_coord = space_index % GY
    below = move_face(own_block[:, :, -1:, :], 1) * (y_coord > 0).astype(own_block.dtype)
    above = move_face(own_block[:, :, :1, :], -1) * (y_coord < GY - 1).astype(own_block.dtype)
    widened = jnp.concatenate([below, own_block, above], axis=2)
    behind = move_face(widened[:, -1:, :, :], GY)
    ahead = move_face(widened[:, :1, :, :], -GY)
    return jnp.concatenate([behind, widened, ahead], axis=1)


def pad_depth(own_block):
    return jnp.pad(own_block, ((1, 1), (0, 0), (0, 0), (0, 0)))


def windows_at(padded, positions):

    def one_window(z_index):
        return lax.dynamic_slice_in_dim(padded, z_index * TE, TE + 2, 0)

    return jax.vmap(one_window)(positions)


def unfold(windows, flipped):
    pieces = []
    for kernel_tap in range(27):
        z_step, x_step, y_step = (kernel_tap // 9, kernel_tap // 3 % 3, kernel_tap % 3)
        if flipped:
            z_step, x_step, y_step = (2 - z_step, 2 - x_step, 2 - y_step)
        pieces.append(
            windows[:, z_step : z_step + TE, x_step : x_step + TE, y_step : y_step + TE, :]
        )
    stacked = jnp.concatenate(pieces, axis=-1)
    return stacked.reshape(-1, stacked.shape[-1])


def tile_sum(columns, delta):
    return lax.dot_general(
        columns, delta, (((0,), (0,)), ((), ())), preferred_element_type=jnp.float32
    )


def on_device(features, cotangent, first_kernel, second_kernel, slot_tile, slot_used):
    depth_index = lax.axis_index("depth")
    space_index = lax.axis_index("space")
    slot_count = features.shape[1]
    voxels = features.shape[2]
    channels = features.shape[3]
    position_count = slot_tile.shape[1]
    placement = place_matrix(slot_tile, slot_used, position_count)
    own_first = depth_index * slot_count
    own_tiles = lax.dynamic_slice_in_dim(slot_tile[0], own_first, slot_count, 0)
    own_used = lax.dynamic_slice_in_dim(slot_used[0], own_first, slot_count, 0).astype(jnp.float32)
    feature_slots = features[0]
    upstream_slots = cotangent[0]

    def column_move(face, offset):
        return from_behind(face, "space", offset)

    def halo_of(tile_rows):
        column = dense_column(tile_rows.reshape(slot_count, voxels, channels), placement)
        return pad_depth(extend_sides(column, column_move, space_index))

    upstream = upstream_slots.reshape(-1, channels)
    source_column = halo_of(feature_slots)
    alive_rows = jnp.repeat(own_used, voxels)[:, None]
    forward_one = first_kernel.reshape(-1, channels)
    forward_two = second_kernel.reshape(-1, channels)
    backward_one = jnp.transpose(first_kernel, (0, 2, 1)).reshape(-1, channels)
    backward_two = jnp.transpose(second_kernel, (0, 2, 1)).reshape(-1, channels)
    source_cols = unfold(windows_at(source_column, own_tiles), False)
    pre_one = jnp.dot(source_cols, forward_one, preferred_element_type=jnp.float32)
    act_value, slope_one = gelu_pair(pre_one)
    act_one = (act_value * alive_rows).astype(jnp.bfloat16)
    act_cols = unfold(windows_at(halo_of(act_one), own_tiles), False)
    pre_two = jnp.dot(act_cols, forward_two, preferred_element_type=jnp.float32)
    slope_two = gelu_slope(pre_two)
    delta_two = (upstream.astype(jnp.float32) * slope_two * alive_rows).astype(jnp.bfloat16)
    second_grad = tile_sum(act_cols, delta_two).reshape(-1) * (1.0 / voxels)
    back_one = jnp.dot(
        unfold(windows_at(halo_of(delta_two), own_tiles), True),
        backward_two,
        preferred_element_type=jnp.float32,
    )
    delta_one = (back_one * slope_one * alive_rows).astype(jnp.bfloat16)
    first_grad = tile_sum(source_cols, delta_one).reshape(-1) * (1.0 / voxels)
    back_zero = jnp.dot(
        unfold(windows_at(halo_of(delta_one), own_tiles), True),
        backward_one,
        preferred_element_type=jnp.float32,
    )
    used_rows = jnp.repeat(own_used, voxels)[:, None]
    input_grad = (back_zero * used_rows).astype(jnp.bfloat16).reshape(features.shape)
    first_share, second_share = (
        lax.psum_scatter(first_grad, ("space", "depth"), scatter_dimension=0, tiled=True),
        lax.psum_scatter(second_grad, ("space", "depth"), scatter_dimension=0, tiled=True),
    )
    return (input_grad, first_share, second_share)


def solution(mesh):
    return jax.shard_map(
        on_device,
        mesh=mesh,
        in_specs=(
            P("space", "depth", None, None),
            P("space", "depth", None, None),
            P(),
            P(),
            P("space", None),
            P("space", None),
        ),
        out_specs=(P("space", "depth", None, None), P(("space", "depth")), P(("space", "depth"))),
        check_vma=False,
    )
```

profile of v0, /device:TPU:1, one launch (start us, length us, event | category | flops | bytes accessed | tf_op | source)
XLA Modules:
  0.0 668.0 jit_solution(10865954893437013768)
XLA Ops:
  7.9 13.4 %all-gather = bf16[4,1,512,128]{3,2,1,0:T(8,128)(2,1)S(1)} all-gather(bf16[1,1,512,128]{3,2,1,0:T(8,128)(2,1)} %param.6), channel_id=2, replica_groups=mesh['space'=128,'depth'=4] {'depth'}, dimensions={0}, use_global_device_ids=true | all-gather | bytes 655360 | tf_op jit(solution)/shard_map/all_gather | solution.py:48
  27.1 3.7 collective-permute-done.1
  31.1 3.0 collective-permute-start.2
  38.3 1.7 collective-permute-done.3
  42.3 2.5 multiply_convert_fusion
  44.8 9.1 %all-gather.1 = bf16[2048,128]{1,0:T(8,128)(2,1)S(1)} all-gather(bf16[512,128]{1,0:T(8,128)(2,1)S(1)} %get-tuple-element.67), channel_id=3, replica_groups=mesh['space'=128,'depth'=4] {'depth'}, dimensions={0}, use_global_device_ids=true | all-gather | bytes 655360 | tf_op jit(solution)/shard_map/all_gather | solution.py:48
  59.1 3.7 collective-permute-done.5
  63.1 9.3 %collective-permute-start.6 = (bf16[32,1,10,128]{3,2,1,0:T(8,128)(2,1)S(1)}, bf16[32,1,10,128]{3,2,1,0:T(8,128)(2,1)S(1)}, u32[]{:S(2)}, u32[]{:S(2)}) collective-permute-start(bf16[32,1,10,128]{3,2,1,0:T(8,128)(2,1)S(1)} %get-tuple-element.55), channel_id=1, source_target_pairs={{0,32},{4,36},{8,40},{12,44},{16,48},{20,52},{24,56},{28,60},{32,6... | collective-permute-start | bytes 245768 | tf_op jit(solution)/shard_map/ppermute | solution.py:17
  74.3 6.3 collective-permute-done.7
  82.9 2.6 fusion.63
  85.6 8.5 %all-gather.2 = bf16[2048,128]{1,0:T(8,128)(2,1)S(1)} all-gather(bf16[512,128]{1,0:T(8,128)(2,1)S(1)} %get-tuple-element.69), channel_id=4, replica_groups=mesh['space'=128,'depth'=4] {'depth'}, dimensions={0}, use_global_device_ids=true | all-gather | bytes 655360 | tf_op jit(solution)/shard_map/all_gather | solution.py:48
  99.2 3.7 collective-permute-done.9
  103.9 10.0 %collective-permute-start.10 = (bf16[32,1,10,128]{3,2,1,0:T(8,128)(2,1)}, bf16[32,1,10,128]{3,2,1,0:T(8,128)(2,1)}, u32[]{:S(2)}, u32[]{:S(2)}) collective-permute-start(bf16[32,1,10,128]{3,2,1,0:T(8,128)(2,1)} %get-tuple-element.53), channel_id=1, source_target_pairs={{0,32},{4,36},{8,40},{12,44},{16,48},{20,52},{24,56},{28,60},{32,6... | collective-permute-start | bytes 245768 | tf_op jit(solution)/shard_map/ppermute | solution.py:17
  115.5 2.3 copy.32
  117.7 2.2 copy.29
  123.6 1.9 fusion.3
  125.5 8.6 %all-gather.3 = bf16[2048,128]{1,0:T(8,128)(2,1)S(1)} all-gather(bf16[512,128]{1,0:T(8,128)(2,1)S(1)} %fusion.3), channel_id=5, replica_groups=mesh['space'=128,'depth'=4] {'depth'}, dimensions={0}, use_global_device_ids=true | all-gather | bytes 655360 | tf_op jit(solution)/shard_map/all_gather | solution.py:48
  136.2 3.2 fusion
  140.8 5.3 collective-permute-done.13
  147.2 10.7 %collective-permute-start.14 = (bf16[32,1,10,128]{3,2,1,0:T(8,128)(2,1)}, bf16[32,1,10,128]{3,2,1,0:T(8,128)(2,1)}, u32[]{:S(2)}, u32[]{:S(2)}) collective-permute-start(bf16[32,1,10,128]{3,2,1,0:T(8,128)(2,1)} %get-tuple-element.51), channel_id=1, source_target_pairs={{0,32},{4,36},{8,40},{12,44},{16,48},{20,52},{24,56},{28,60},{32,6... | collective-permute-start | bytes 245768 | tf_op jit(solution)/shard_map/ppermute | solution.py:17
  159.2 2.4 fusion.1
  161.6 2.3 collective-permute-done.15
  167.2 2.4 fusion.5
  169.6 488.8 %all-reduce.9.cloned.1.call-done = (f32[442368]{0:T(1024)}, f32[442368]{0:T(1024)}) async-done(((f32[442368]{0:T(1024)}, f32[442368]{0:T(1024)}), (f32[442368]{0:T(1024)}, f32[442368]{0:T(1024)})) %all-reduce.9.cloned.1.call-update) | async-done | bytes 3538960
  (203 shorter events, 43.3 us)
Async XLA Ops:
  7.2 28.6 %copy-start.17 = (s32[1,4]{1,0:T(1,128)S(1)}, s32[1,4]{1,0:T(1,128)}, u32[]{:S(2)}) copy-start(s32[1,4]{1,0:T(1,128)} %param.11) | copy-start | bytes 52
  7.2 28.6 %copy-start.16 = (s32[1,4]{1,0:T(1,128)S(1)}, s32[1,4]{1,0:T(1,128)}, u32[]{:S(2)}) copy-start(s32[1,4]{1,0:T(1,128)} %param.10) | copy-start | bytes 52
  7.2 651.2 %all-reduce.9.cloned.1.call-start = ((), (), s32[]{:S(2)}) async-start(), calls=%async_computation | async-start | bytes 7077888
  22.7 4.2 collective-permute-start
  24.0 6.8 %collective-permute-start.1 = (bf16[32,8,1,128]{3,2,1,0:T(2,128)(2,1)S(1)}, bf16[32,8,1,128]{3,2,1,0:T(2,128)(2,1)S(1)}, u32[]{:S(2)}, u32[]{:S(2)}) collective-permute-start(bf16[32,8,1,128]{3,2,1,0:T(2,128)(2,1)S(1)} %get-tuple-element.66), channel_id=1, source_target_pairs={{4,0},{8,4},{12,8},{16,12},{20,16},{24,20},{28,24},{32,28},{36,32}... | collective-permute-start | bytes 196616 | tf_op jit(solution)/shard_map/ppermute | solution.py:17
  31.1 7.2 %collective-permute-start.2 = (bf16[32,1,10,128]{3,2,1,0:T(8,128)(2,1)S(1)}, bf16[32,1,10,128]{3,2,1,0:T(8,128)(2,1)S(1)}, u32[]{:S(2)}, u32[]{:S(2)}) collective-permute-start(bf16[32,1,10,128]{3,2,1,0:T(8,128)(2,1)S(1)} %get-tuple-element.57), channel_id=1, source_target_pairs={{0,32},{4,36},{8,40},{12,44},{16,48},{20,52},{24,56},{28,60},{32,6... | collective-permute-start | bytes 245768 | tf_op jit(solution)/shard_map/ppermute | solution.py:17
  34.1 5.9 collective-permute-start.3
  40.6 40.1 %copy-start.4 = (pred[10,10,10,128]{3,2,1,0:T(8,128)(4,1)}, pred[10,10,10,128]{3,2,1,0:T(8,128)(4,1)S(1)}, u32[]{:S(2)}) copy-start(pred[10,10,10,128]{3,2,1,0:T(8,128)(4,1)S(1)} %get-tuple-element.50) | copy-start | bytes 384004
  54.7 4.3 collective-permute-start.4
  56.0 6.8 %collective-permute-start.5 = (bf16[32,8,1,128]{3,2,1,0:T(2,128)(2,1)S(1)}, bf16[32,8,1,128]{3,2,1,0:T(2,128)(2,1)S(1)}, u32[]{:S(2)}, u32[]{:S(2)}) collective-permute-start(bf16[32,8,1,128]{3,2,1,0:T(2,128)(2,1)S(1)} %get-tuple-element.64), channel_id=1, source_target_pairs={{4,0},{8,4},{12,8},{16,12},{20,16},{24,20},{28,24},{32,28},{36,32}... | collective-permute-start | bytes 196616 | tf_op jit(solution)/shard_map/ppermute | solution.py:17
  63.1 11.2 %collective-permute-start.6 = (bf16[32,1,10,128]{3,2,1,0:T(8,128)(2,1)S(1)}, bf16[32,1,10,128]{3,2,1,0:T(8,128)(2,1)S(1)}, u32[]{:S(2)}, u32[]{:S(2)}) collective-permute-start(bf16[32,1,10,128]{3,2,1,0:T(8,128)(2,1)S(1)} %get-tuple-element.55), channel_id=1, source_target_pairs={{0,32},{4,36},{8,40},{12,44},{16,48},{20,52},{24,56},{28,60},{32,6... | collective-permute-start | bytes 245768 | tf_op jit(solution)/shard_map/ppermute | solution.py:17
  72.4 8.2 %collective-permute-start.7 = (bf16[32,1,10,128]{3,2,1,0:T(8,128)(2,1)S(1)}, bf16[32,1,10,128]{3,2,1,0:T(8,128)(2,1)S(1)}, u32[]{:S(2)}, u32[]{:S(2)}) collective-permute-start(bf16[32,1,10,128]{3,2,1,0:T(8,128)(2,1)S(1)} %get-tuple-element.56), channel_id=1, source_target_pairs={{32,0},{36,4},{40,8},{44,12},{48,16},{52,20},{56,24},{60,28},{64,3... | collective-permute-start | bytes 245768 | tf_op jit(solution)/shard_map/ppermute | solution.py:17
  82.9 11.6 %copy-start.2 = (bf16[1,8,8,8,3456]{4,3,2,1,0:T(8,128)(2,1)}, bf16[1,8,8,8,3456]{4,3,2,1,0:T(8,128)(2,1)S(1)}, u32[]{:S(2)}) copy-start(bf16[1,8,8,8,3456]{4,3,2,1,0:T(8,128)(2,1)S(1)} %constant_dynamic-update-slice_fusion.27) | copy-start | bytes 10616836
  94.8 4.3 collective-permute-start.8
  96.1 6.8 %collective-permute-start.9 = (bf16[32,8,1,128]{3,2,1,0:T(2,128)(2,1)S(1)}, bf16[32,8,1,128]{3,2,1,0:T(2,128)(2,1)S(1)}, u32[]{:S(2)}, u32[]{:S(2)}) collective-permute-start(bf16[32,8,1,128]{3,2,1,0:T(2,128)(2,1)S(1)} %get-tuple-element.62), channel_id=1, source_target_pairs={{4,0},{8,4},{12,8},{16,12},{20,16},{24,20},{28,24},{32,28},{36,32}... | collective-permute-start | bytes 196616 | tf_op jit(solution)/shard_map/ppermute | solution.py:17
  103.9 16.0 %collective-permute-start.10 = (bf16[32,1,10,128]{3,2,1,0:T(8,128)(2,1)}, bf16[32,1,10,128]{3,2,1,0:T(8,128)(2,1)}, u32[]{:S(2)}, u32[]{:S(2)}) collective-permute-start(bf16[32,1,10,128]{3,2,1,0:T(8,128)(2,1)} %get-tuple-element.53), channel_id=1, source_target_pairs={{0,32},{4,36},{8,40},{12,44},{16,48},{20,52},{24,56},{28,60},{32,6... | collective-permute-start | bytes 245768 | tf_op jit(solution)/shard_map/ppermute | solution.py:17
  114.0 6.2 collective-permute-start.11
  123.5 12.7 %copy-start.3 = (bf16[1,8,8,8,3456]{4,3,2,1,0:T(8,128)(2,1)S(1)}, bf16[1,8,8,8,3456]{4,3,2,1,0:T(8,128)(2,1)}, u32[]{:S(2)}) copy-start(bf16[1,8,8,8,3456]{4,3,2,1,0:T(8,128)(2,1)} %copy-done.2) | copy-start | bytes 10616836
  123.5 12.7 %copy-start.13 = (f32[512,128]{1,0:T(8,128)S(1)}, f32[512,128]{1,0:T(8,128)}, u32[]{:S(2)}) copy-start(f32[512,128]{1,0:T(8,128)} %get-tuple-element.70) | copy-start | bytes 786436
  123.5 12.7 %copy-start.15 = (bf16[1,1,512,128]{3,2,1,0:T(8,128)(2,1)S(1)}, bf16[1,1,512,128]{3,2,1,0:T(8,128)(2,1)}, u32[]{:S(2)}) copy-start(bf16[1,1,512,128]{3,2,1,0:T(8,128)(2,1)} %param.7) | copy-start | bytes 393220
  134.9 5.8 collective-permute-start.12
  139.4 6.8 %collective-permute-start.13 = (bf16[32,8,1,128]{3,2,1,0:T(2,128)(2,1)S(1)}, bf16[32,8,1,128]{3,2,1,0:T(2,128)(2,1)S(1)}, u32[]{:S(2)}, u32[]{:S(2)}) collective-permute-start(bf16[32,8,1,128]{3,2,1,0:T(2,128)(2,1)S(1)} %get-tuple-element.60), channel_id=1, source_target_pairs={{4,0},{8,4},{12,8},{16,12},{20,16},{24,20},{28,24},{32,28},{36,32}... | collective-permute-start | bytes 196616 | tf_op jit(solution)/shard_map/ppermute | solution.py:17
  147.2 14.4 %collective-permute-start.14 = (bf16[32,1,10,128]{3,2,1,0:T(8,128)(2,1)}, bf16[32,1,10,128]{3,2,1,0:T(8,128)(2,1)}, u32[]{:S(2)}, u32[]{:S(2)}) collective-permute-start(bf16[32,1,10,128]{3,2,1,0:T(8,128)(2,1)} %get-tuple-element.51), channel_id=1, source_target_pairs={{0,32},{4,36},{8,40},{12,44},{16,48},{20,52},{24,56},{28,60},{32,6... | collective-permute-start | bytes 245768 | tf_op jit(solution)/shard_map/ppermute | solution.py:17
  157.9 6.0 collective-permute-start.15
  (12 other events, 43.5 us)
Sparse Core Ops, SparseCore 0:
  161.7 496.6 all-reduce.8
where the time goes:
time: 669 us; the launch traced here: 668 us
  waiting for transfers between devices  521 us (78%)
  starting transfers between devices  48.8 us (7%)
  blocking collectives  39.6 us (6%)
  between operations  17.1 us (3%)
  matrix products  16.9 us (3%)
  local copies, waits for them, and re-layouts  14.8 us (2%)
  other arithmetic  9.57 us (1%)
    unnamed x2, waiting for transfers between devices  489 us
    ppermute x16, starting transfers between devices, from_behind(): return lax.ppermute(block, axis, route)  48.7 us
    all_gather x4, blocking collectives, dense_column(): lax.all_gather(tile_rows, 'depth', axis=0, tiled=True)  39.6 us
    ppermute x16, waiting for transfers between devices, from_behind(): return lax.ppermute(block, axis, route)  32.4 us
    unnamed x146, local copies, waits for them, and re-layouts  13.6 us
  transfers between devices with their start and end apart: 17, of which 13 were waited for; matrix products, arithmetic and copies ran while one was open for 3% of the time, Pallas kernels for 0%

commit v1 on v0

--- a/solution.py
+++ b/solution.py
@@ -1,7 +1,13 @@
+import functools
+
 import jax
 import jax.numpy as jnp
 from jax import lax
+from jax.experimental import pallas as pl
+from jax.experimental.pallas import tpu as pltpu
 from jax.sharding import PartitionSpec as P
+
+MESH = pl.DeviceIdType.MESH
 
 TE = 8
 GY = 8
@@ -90,6 +96,249 @@
     return lax.dot_general(
         columns, delta, (((0,), (0,)), ((), ())), preferred_element_type=jnp.float32
     )
+
+
+PLANE = 16
+DEEP = 16
+PIECE = 8
+
+
+def far_first(step, count):
+    half = count // 2
+    return half + (step + 1) // 2 * (1 - 2 * (step % 2))
+
+
+class Spot:
+
+    def __init__(self):
+        space = lax.axis_index("space")
+        self.depth = lax.axis_index("depth")
+        self.space = space
+        self.z = space // 8
+        self.column = space % 8
+        self.core = self.depth % 2
+        self.x_lo = self.depth // 2
+        self.plane = self.column * 2 + self.x_lo
+
+    def plane_peer(self, rank):
+        return (self.z * 8 + rank // 2, rank % 2 * 2 + self.core)
+
+    def deep_peer(self, rank):
+        return (rank * 8 + self.column, self.depth)
+
+    def column_peer(self, rank):
+        return (self.space, rank)
+
+
+def greet(spot):
+    barrier = pltpu.get_barrier_semaphore()
+
+    def tell(peer):
+        pl.semaphore_signal(barrier, inc=1, device_id=peer, device_id_type=MESH)
+
+    tell(spot.column_peer(spot.x_lo * 2 + 1 - spot.core))
+    tell(spot.column_peer((1 - spot.x_lo) * 2 + 1 - spot.core))
+
+    @pl.loop(0, 15)
+    def _(step):
+        tell(spot.deep_peer((spot.z + far_first(step, 16)) % 16))
+
+    @pl.loop(0, 15)
+    def _(step):
+        tell(spot.plane_peer((spot.plane + step + 1) % 16))
+
+    pl.semaphore_wait(barrier, 32)
+
+
+def send(source, target, send_sem, recv_sem, peer):
+    return pltpu.make_async_remote_copy(
+        src_ref=source, dst_ref=target, send_sem=send_sem, recv_sem=recv_sem, device_id=peer, device_id_type=MESH
+    )
+
+
+class Scatter:
+
+    def __init__(self, spot, refs):
+        self.spot = spot
+        (self.halves, self.partner, self.merged, self.plane_in, self.deep_out, self.deep_in, self.pieces, self.sems,
+         self.plane_sems, self.deep_sems, self.piece_sems) = refs
+
+    @staticmethod
+    def scratch():
+        return [
+            pltpu.VMEM((2, PLANE, DEEP, PIECE, 128), jnp.bfloat16),
+            pltpu.VMEM((PLANE, DEEP, PIECE, 128), jnp.bfloat16),
+            pltpu.VMEM((PLANE, DEEP, PIECE, 128), jnp.bfloat16),
+            pltpu.VMEM((PLANE, DEEP, PIECE, 128), jnp.bfloat16),
+            pltpu.VMEM((DEEP, PIECE, 128), jnp.float32),
+            pltpu.VMEM((DEEP, PIECE, 128), jnp.float32),
+            pltpu.VMEM((4, PIECE, 128), jnp.float32),
+            pltpu.SemaphoreType.DMA((2,)),
+            pltpu.SemaphoreType.DMA((2, 16)),
+            pltpu.SemaphoreType.DMA((2, 16)),
+            pltpu.SemaphoreType.DMA((2, 4)),
+        ]
+
+    def cut(self, grad_ref):
+
+        @pl.loop(0, DEEP)
+        def _(z):
+            rows = grad_ref[pl.ds(pl.multiple_of(z * 216, 8), 216), :]
+            rows = jnp.concatenate([rows, jnp.zeros((8, 128), jnp.float32)], axis=0)
+            for column in range(8):
+                for part in range(4):
+                    first = column * 27 + part * 8
+                    self.halves[part % 2, column * 2 + part // 2, z] = rows[first : first + 8].astype(jnp.bfloat16)
+
+    def pair_copy(self):
+        spot = self.spot
+        other = 1 - spot.core
+        return send(self.halves.at[other], self.partner, self.sems.at[0], self.sems.at[1],
+                    spot.column_peer(spot.x_lo * 2 + other))
+
+    def merge(self):
+        core = self.spot.core
+
+        @pl.loop(0, PLANE)
+        def _(rank):
+            both = self.halves[core, rank].astype(jnp.float32) + self.partner[rank].astype(jnp.float32)
+            self.merged[rank] = both.astype(jnp.bfloat16)
+
+    def plane_copy(self, step):
+        me = self.spot.plane
+        rank = (me + step) % PLANE
+        return send(self.merged.at[rank], self.plane_in.at[me], self.plane_sems.at[0, rank], self.plane_sems.at[1, me],
+                    self.spot.plane_peer(rank))
+
+    def plane_arrival(self, step):
+        me = self.spot.plane
+        rank = (me + step) % PLANE
+        return send(self.merged.at[rank], self.plane_in.at[rank], self.plane_sems.at[0, rank],
+                    self.plane_sems.at[1, rank], self.spot.plane_peer(rank))
+
+    def plane_start(self):
+
+        @pl.loop(1, PLANE)
+        def _(step):
+            self.plane_copy(step).start()
+
+    def plane_finish(self):
+        me = self.spot.plane
+        self.plane_in[me] = self.merged[me]
+
+        @pl.loop(1, PLANE)
+        def _(step):
+            self.plane_arrival(step).wait_recv()
+
+        @pl.loop(0, DEEP)
+        def _(z):
+            total = jnp.zeros((PIECE, 128), jnp.float32)
+            for rank in range(PLANE):
+                total = total + self.plane_in[rank, z].astype(jnp.float32)
+            self.deep_out[z] = total
+
+    def deep_copy(self, step):
+        me = self.spot.z
+        rank = (me + far_first(step, DEEP)) % DEEP
+        return send(self.deep_out.at[rank], self.deep_in.at[me], self.deep_sems.at[0, rank], self.deep_sems.at[1, me],
+                    self.spot.deep_peer(rank))
+
+    def deep_arrival(self, step):
+        me = self.spot.z
+        rank = (me + far_first(step, DEEP)) % DEEP
+        return send(self.deep_out.at[rank], self.deep_in.at[rank], self.deep_sems.at[0, rank],
+                    self.deep_sems.at[1, rank], self.spot.deep_peer(rank))
+
+    def deep_start(self):
+
+        @pl.loop(0, DEEP - 1)
+        def _(step):
+            self.deep_copy(step).start()
+
+    def deep_finish(self):
+        me = self.spot.z
+        self.deep_in[me] = self.deep_out[me]
+
+        @pl.loop(0, DEEP - 1)
+        def _(step):
+            self.deep_arrival(step).wait_recv()
+
+        total = jnp.zeros((PIECE, 128), jnp.float32)
+        for rank in range(DEEP):
+            total = total + self.deep_in[rank]
+        self.pieces[self.spot.depth] = total * (1.0 / 512)
+
+    def piece_copy(self, step):
+        me = self.spot.depth
+        rank = (me + step) % 4
+        return send(self.pieces.at[me], self.pieces.at[me], self.piece_sems.at[0, rank], self.piece_sems.at[1, me],
+                    self.spot.column_peer(rank))
+
+    def piece_arrival(self, step):
+        me = self.spot.depth
+        rank = (me + step) % 4
+        return send(self.pieces.at[rank], self.pieces.at[rank], self.piece_sems.at[0, rank],
+                    self.piece_sems.at[1, rank], self.spot.column_peer(rank))
+
+    def piece_start(self):
+        for step in range(1, 4):
+            self.piece_copy(step).start()
+
+    def piece_finish(self, out_ref):
+        for step in range(1, 4):
+            self.piece_arrival(step).wait_recv()
+        for rank in range(4):
+            out_ref[rank] = self.pieces[rank]
+
+    def drain(self):
+        self.pair_copy().wait_send()
+
+        @pl.loop(1, PLANE)
+        def _(step):
+            self.plane_copy(step).wait_send()
+
+        @pl.loop(0, DEEP - 1)
+        def _(step):
+            self.deep_copy(step).wait_send()
+
+        for step in range(1, 4):
+            self.piece_copy(step).wait_send()
+
+
+def scatter_kernel(one_ref, two_ref, out_one, out_two, *scratch):
+    spot = Spot()
+    count = len(scratch) // 2
+    pair = [(Scatter(spot, scratch[count:]), two_ref, out_two), (Scatter(spot, scratch[:count]), one_ref, out_one)]
+    greet(spot)
+    for scatter, grad, _ in pair:
+        scatter.cut(grad)
+        scatter.pair_copy().start()
+    for scatter, _, _ in pair:
+        scatter.pair_copy().wait_recv()
+        scatter.merge()
+        scatter.plane_start()
+    for scatter, _, _ in pair:
+        scatter.plane_finish()
+        scatter.deep_start()
+    for scatter, _, _ in pair:
+        scatter.deep_finish()
+        scatter.piece_start()
+    for scatter, _, out in pair:
+        scatter.piece_finish(out)
+    for scatter, _, _ in pair:
+        scatter.drain()
+
+
+def scatter_both(one, two):
+    shape = jax.ShapeDtypeStruct((4, PIECE, 128), jnp.float32)
+    return pl.pallas_call(
+        scatter_kernel,
+        out_shape=(shape, shape),
+        in_specs=[pl.BlockSpec(memory_space=pltpu.VMEM)] * 2,
+        out_specs=(pl.BlockSpec(memory_space=pltpu.VMEM),) * 2,
+        scratch_shapes=Scatter.scratch() * 2,
+        compiler_params=pltpu.CompilerParams(collective_id=0, has_side_effects=True, vmem_limit_bytes=40 << 20),
+    )(one, two)
 
 
 def on_device(features, cotangent, first_kernel, second_kernel, slot_tile, slot_used):
@@ -128,14 +377,14 @@
     pre_two = jnp.dot(act_cols, forward_two, preferred_element_type=jnp.float32)
     slope_two = gelu_slope(pre_two)
     delta_two = (upstream.astype(jnp.float32) * slope_two * alive_rows).astype(jnp.bfloat16)
-    second_grad = tile_sum(act_cols, delta_two).reshape(-1) * (1.0 / voxels)
+    second_grad = tile_sum(act_cols, delta_two)
     back_one = jnp.dot(
         unfold(windows_at(halo_of(delta_two), own_tiles), True),
         backward_two,
         preferred_element_type=jnp.float32,
     )
     delta_one = (back_one * slope_one * alive_rows).astype(jnp.bfloat16)
-    first_grad = tile_sum(source_cols, delta_one).reshape(-1) * (1.0 / voxels)
+    first_grad = tile_sum(source_cols, delta_one)
     back_zero = jnp.dot(
         unfold(windows_at(halo_of(delta_one), own_tiles), True),
         backward_one,
@@ -143,10 +392,13 @@
     )
     used_rows = jnp.repeat(own_used, voxels)[:, None]
     input_grad = (back_zero * used_rows).astype(jnp.bfloat16).reshape(features.shape)
-    first_share, second_share = (
-        lax.psum_scatter(first_grad, ("space", "depth"), scatter_dimension=0, tiled=True),
-        lax.psum_scatter(second_grad, ("space", "depth"), scatter_dimension=0, tiled=True),
-    )
+    first_sum, second_sum = scatter_both(first_grad, second_grad)
+    own_share = 27 * channels // 4
+
+    def share(total):
+        return lax.dynamic_slice_in_dim(total.reshape(-1), depth_index * own_share, own_share, 0)
+
+    first_share, second_share = (share(first_sum), share(second_sum))
     return (input_grad, first_share, second_share)
 
 

time: 669 us -> 201 us (0.30)
  waiting for transfers between devices: 521 us -> 30.2 us
  Pallas kernels: 0 us -> 44.1 us
  between operations: 17.1 us -> 3.73 us
    unnamed x2 -> x0, waiting for transfers between devices: 489 us -> none
    pallas_call x0 -> x1, Pallas kernels: none -> 44.1 us  [scatter_both(): pl.pallas_call(scatter_kernel, out_shape=(shape, shape), in_specs=[pl.Blo...]
    unnamed x146 -> x140, local copies, waits for them, and re-layouts: 13.6 us -> 10.8 us
  transfers between devices with their start and end apart: 17 -> 16, of which waited for: 13 -> 11; matrix products, arithmetic and copies ran while one was open for 3% -> 5% of each run, Pallas kernels for 0% -> 22%
where the time goes in v1:
time: 201 us
  starting transfers between devices  48.1 us (24%)
  Pallas kernels  44.1 us (22%)
  blocking collectives  39.6 us (20%)
  waiting for transfers between devices  30.2 us (15%)
  matrix products  13.9 us (7%)
  local copies, waits for them, and re-layouts  13.3 us (7%)
  other arithmetic  7.82 us (4%)
  between operations  3.73 us (2%)
    ppermute x16, starting transfers between devices, from_behind(): return lax.ppermute(block, axis, route)  48.1 us
    pallas_call x1, Pallas kernels, scatter_both(): pl.pallas_call(scatter_kernel, out_shape=(shape, shape), in_specs=[pl.Blo...  44.1 us
    all_gather x4, blocking collectives, dense_column(): lax.all_gather(tile_rows, 'depth', axis=0, tiled=True)  39.6 us
    ppermute x16, waiting for transfers between devices, from_behind(): return lax.ppermute(block, axis, route)  30.2 us
    unnamed x140, local copies, waits for them, and re-layouts  10.8 us
  transfers between devices with their start and end apart: 16, of which 11 were waited for; matrix products, arithmetic and copies ran while one was open for 5% of the time, Pallas kernels for 22%

profile of v1, /device:TPU:1, one launch (start us, length us, event | category | flops | bytes accessed | tf_op | source)
XLA Modules:
  0.0 200.8 jit_solution(5424512780823675405)
XLA Ops:
  1.4 13.4 %all-gather = bf16[4,1,512,128]{3,2,1,0:T(8,128)(2,1)S(1)} all-gather(bf16[1,1,512,128]{3,2,1,0:T(8,128)(2,1)} %param.6), channel_id=2, replica_groups=mesh['space'=128,'depth'=4] {'depth'}, dimensions={0}, use_global_device_ids=true | all-gather | bytes 655360 | tf_op jit(solution)/shard_map/all_gather | solution.py:54
  20.5 3.7 %collective-permute-done.1 = bf16[32,8,1,128]{3,2,1,0:T(2,128)(2,1)S(1)} collective-permute-done((bf16[32,8,1,128]{3,2,1,0:T(2,128)(2,1)S(1)}, bf16[32,8,1,128]{3,2,1,0:T(2,128)(2,1)S(1)}, u32[]{:S(2)}, u32[]{:S(2)}) %collective-permute-start.1) | collective-permute-done | bytes 65568 | tf_op jit(solution)/shard_map/ppermute | solution.py:23
  24.5 3.0 %collective-permute-start.2 = (bf16[32,1,10,128]{3,2,1,0:T(8,128)(2,1)S(1)}, bf16[32,1,10,128]{3,2,1,0:T(8,128)(2,1)S(1)}, u32[]{:S(2)}, u32[]{:S(2)}) collective-permute-start(bf16[32,1,10,128]{3,2,1,0:T(8,128)(2,1)S(1)} %get-tuple-element.59), channel_id=1, source_target_pairs={{0,32},{4,36},{8,40},{12,44},{16,48},{20,52},{24,56},{28,60},{32,6... | collective-permute-start | bytes 245768 | tf_op jit(solution)/shard_map/ppermute | solution.py:23
  31.8 1.7 collective-permute-done.3
  35.8 2.4 %multiply_convert_fusion = (bf16[512,128]{1,0:T(8,128)(2,1)S(1)}, f32[512,128]{1,0:T(8,128)}) fusion(f32[]{:T(128)} %bitcast.11, bf16[512,3456]{1,0:T(8,128)(2,1)S(1)} %bitcast.66, bf16[3456,128]{1,0:T(8,128)(2,1)S(1)} %bitcast.82), kind=kOutput, calls=%fused_computation.100 | convolution fusion | flops 453640192 | bytes 4816900 | tf_op jit(solution)/shard_map/dot_general | solution.py:373
  38.2 9.1 %all-gather.1 = bf16[2048,128]{1,0:T(8,128)(2,1)S(1)} all-gather(bf16[512,128]{1,0:T(8,128)(2,1)S(1)} %get-tuple-element.69), channel_id=3, replica_groups=mesh['space'=128,'depth'=4] {'depth'}, dimensions={0}, use_global_device_ids=true | all-gather | bytes 655360 | tf_op jit(solution)/shard_map/all_gather | solution.py:54
  50.7 1.6 collective-permute-done.4
  52.5 3.7 %collective-permute-done.5 = bf16[32,8,1,128]{3,2,1,0:T(2,128)(2,1)S(1)} collective-permute-done((bf16[32,8,1,128]{3,2,1,0:T(2,128)(2,1)S(1)}, bf16[32,8,1,128]{3,2,1,0:T(2,128)(2,1)S(1)}, u32[]{:S(2)}, u32[]{:S(2)}) %collective-permute-start.5) | collective-permute-done | bytes 65568 | tf_op jit(solution)/shard_map/ppermute | solution.py:23
  56.5 9.3 %collective-permute-start.6 = (bf16[32,1,10,128]{3,2,1,0:T(8,128)(2,1)S(1)}, bf16[32,1,10,128]{3,2,1,0:T(8,128)(2,1)S(1)}, u32[]{:S(2)}, u32[]{:S(2)}) collective-permute-start(bf16[32,1,10,128]{3,2,1,0:T(8,128)(2,1)S(1)} %get-tuple-element.57), channel_id=1, source_target_pairs={{0,32},{4,36},{8,40},{12,44},{16,48},{20,52},{24,56},{28,60},{32,6... | collective-permute-start | bytes 245768 | tf_op jit(solution)/shard_map/ppermute | solution.py:23
  67.7 6.3 %collective-permute-done.7 = bf16[32,1,10,128]{3,2,1,0:T(8,128)(2,1)S(1)} collective-permute-done((bf16[32,1,10,128]{3,2,1,0:T(8,128)(2,1)S(1)}, bf16[32,1,10,128]{3,2,1,0:T(8,128)(2,1)S(1)}, u32[]{:S(2)}, u32[]{:S(2)}) %collective-permute-start.7) | collective-permute-done | bytes 81952 | tf_op jit(solution)/shard_map/ppermute | solution.py:23
  76.3 2.5 %fusion.61 = (bf16[512,128]{1,0:T(8,128)(2,1)S(1)}, f32[512,128]{1,0:T(8,128)}) fusion(bf16[1,1,512,128]{3,2,1,0:T(8,128)(2,1)S(1)} %copy-done.12, f32[]{:T(128)} %bitcast.11, bf16[512,3456]{1,0:T(8,128)(2,1)S(1)} %bitcast.80, bf16[3456,128]{1,0:T(8,128)(2,1)S(1)} %bitcast.83), kind=kOutput, calls=%fused_computation.95 | convolution fusion | flops 454361088 | bytes 4947972 | tf_op jit(solution)/shard_map/dot_general | solution.py:377
  78.8 8.5 %all-gather.2 = bf16[2048,128]{1,0:T(8,128)(2,1)S(1)} all-gather(bf16[512,128]{1,0:T(8,128)(2,1)S(1)} %get-tuple-element.71), channel_id=4, replica_groups=mesh['space'=128,'depth'=4] {'depth'}, dimensions={0}, use_global_device_ids=true | all-gather | bytes 655360 | tf_op jit(solution)/shard_map/all_gather | solution.py:54
  90.7 1.6 collective-permute-done.8
  92.5 3.7 %collective-permute-done.9 = bf16[32,8,1,128]{3,2,1,0:T(2,128)(2,1)S(1)} collective-permute-done((bf16[32,8,1,128]{3,2,1,0:T(2,128)(2,1)S(1)}, bf16[32,8,1,128]{3,2,1,0:T(2,128)(2,1)S(1)}, u32[]{:S(2)}, u32[]{:S(2)}) %collective-permute-start.9) | collective-permute-done | bytes 65568 | tf_op jit(solution)/shard_map/ppermute | solution.py:23
  97.2 10.0 %collective-permute-start.10 = (bf16[32,1,10,128]{3,2,1,0:T(8,128)(2,1)}, bf16[32,1,10,128]{3,2,1,0:T(8,128)(2,1)}, u32[]{:S(2)}, u32[]{:S(2)}) collective-permute-start(bf16[32,1,10,128]{3,2,1,0:T(8,128)(2,1)} %get-tuple-element.55), channel_id=1, source_target_pairs={{0,32},{4,36},{8,40},{12,44},{16,48},{20,52},{24,56},{28,60},{32,6... | collective-permute-start | bytes 245768 | tf_op jit(solution)/shard_map/ppermute | solution.py:23
  108.6 2.2 %copy.32 = bf16[27,128,128]{1,2,0:T(8,128)(2,1)} copy(bf16[27,128,128]{2,1,0:T(8,128)(2,1)} %param.8) | data formatting | bytes 1769472 | tf_op args[2]
  110.9 2.2 %copy.29 = bf16[27,128,128]{1,2,0:T(8,128)(2,1)} copy(bf16[27,128,128]{2,1,0:T(8,128)(2,1)} %param.9) | data formatting | bytes 1769472 | tf_op args[3]
  116.8 1.8 fusion.1
  118.6 8.6 %all-gather.3 = bf16[2048,128]{1,0:T(8,128)(2,1)S(1)} all-gather(bf16[512,128]{1,0:T(8,128)(2,1)S(1)} %fusion.1), channel_id=5, replica_groups=mesh['space'=128,'depth'=4] {'depth'}, dimensions={0}, use_global_device_ids=true | all-gather | bytes 655360 | tf_op jit(solution)/shard_map/all_gather | solution.py:54
  129.3 1.8 fusion.65.two_ref
  132.6 5.3 %collective-permute-done.13 = bf16[32,8,1,128]{3,2,1,0:T(2,128)(2,1)S(1)} collective-permute-done((bf16[32,8,1,128]{3,2,1,0:T(2,128)(2,1)S(1)}, bf16[32,8,1,128]{3,2,1,0:T(2,128)(2,1)S(1)}, u32[]{:S(2)}, u32[]{:S(2)}) %collective-permute-start.13) | collective-permute-done | bytes 65568 | tf_op jit(solution)/shard_map/ppermute | solution.py:23
  138.2 10.1 %collective-permute-start.14 = (bf16[32,1,10,128]{3,2,1,0:T(8,128)(2,1)S(1)}, bf16[32,1,10,128]{3,2,1,0:T(8,128)(2,1)S(1)}, u32[]{:S(2)}, u32[]{:S(2)}) collective-permute-start(bf16[32,1,10,128]{3,2,1,0:T(8,128)(2,1)S(1)} %get-tuple-element.53), channel_id=1, source_target_pairs={{0,32},{4,36},{8,40},{12,44},{16,48},{20,52},{24,56},{28,60},{32,6... | collective-permute-start | bytes 245768 | tf_op jit(solution)/shard_map/ppermute | solution.py:23
  150.8 44.1 %shard_map.85 = (f32[4,8,128]{2,1,0:T(8,128)S(1)}, f32[4,8,128]{2,1,0:T(8,128)S(1)}) custom-call(f32[3456,128]{1,0:T(8,128)S(1)} %fusion.87.one_ref, f32[3456,128]{1,0:T(8,128)S(1)} %fusion.65.two_ref), custom_call_target="tpu_custom_call" | custom-call | tf_op jit(solution)/shard_map/pallas_call | solution.py:334
  198.5 2.3 %fusion.3 = bf16[1,1,512,128]{3,2,1,0:T(8,128)(2,1)} fusion(bf16[512,3456]{1,0:T(8,128)(2,1)S(1)} %bitcast.90, bf16[3456,128]{1,0:T(8,128)(2,1)S(1)} %bitcast.84, f32[]{:T(128)} %bitcast.11), kind=kOutput, calls=%fused_computation.31 | convolution fusion | flops 453115904 | bytes 4554756 | tf_op jit(solution)/shard_map/dot_general | solution.py:388
  (197 shorter events, 38.0 us)
Async XLA Ops:
  0.6 28.6 %copy-start.15 = (s32[1,4]{1,0:T(1,128)S(1)}, s32[1,4]{1,0:T(1,128)}, u32[]{:S(2)}) copy-start(s32[1,4]{1,0:T(1,128)} %param.11) | copy-start | bytes 52
  0.6 28.6 %copy-start.14 = (s32[1,4]{1,0:T(1,128)S(1)}, s32[1,4]{1,0:T(1,128)}, u32[]{:S(2)}) copy-start(s32[1,4]{1,0:T(1,128)} %param.10) | copy-start | bytes 52
  16.2 4.2 %collective-permute-start = (bf16[32,8,1,128]{3,2,1,0:T(2,128)(2,1)S(1)}, bf16[32,8,1,128]{3,2,1,0:T(2,128)(2,1)S(1)}, u32[]{:S(2)}, u32[]{:S(2)}) collective-permute-start(bf16[32,8,1,128]{3,2,1,0:T(2,128)(2,1)S(1)} %get-tuple-element.67), channel_id=1, source_target_pairs={{0,4},{4,8},{8,12},{12,16},{16,20},{20,24},{24,28},{28,32},{32,36}... | collective-permute-start | bytes 196616 | tf_op jit(solution)/shard_map/ppermute | solution.py:23
  17.5 6.8 %collective-permute-start.1 = (bf16[32,8,1,128]{3,2,1,0:T(2,128)(2,1)S(1)}, bf16[32,8,1,128]{3,2,1,0:T(2,128)(2,1)S(1)}, u32[]{:S(2)}, u32[]{:S(2)}) collective-permute-start(bf16[32,8,1,128]{3,2,1,0:T(2,128)(2,1)S(1)} %get-tuple-element.68), channel_id=1, source_target_pairs={{4,0},{8,4},{12,8},{16,12},{20,16},{24,20},{28,24},{32,28},{36,32}... | collective-permute-start | bytes 196616 | tf_op jit(solution)/shard_map/ppermute | solution.py:23
  24.5 7.2 %collective-permute-start.2 = (bf16[32,1,10,128]{3,2,1,0:T(8,128)(2,1)S(1)}, bf16[32,1,10,128]{3,2,1,0:T(8,128)(2,1)S(1)}, u32[]{:S(2)}, u32[]{:S(2)}) collective-permute-start(bf16[32,1,10,128]{3,2,1,0:T(8,128)(2,1)S(1)} %get-tuple-element.59), channel_id=1, source_target_pairs={{0,32},{4,36},{8,40},{12,44},{16,48},{20,52},{24,56},{28,60},{32,6... | collective-permute-start | bytes 245768 | tf_op jit(solution)/shard_map/ppermute | solution.py:23
  27.6 5.9 %collective-permute-start.3 = (bf16[32,1,10,128]{3,2,1,0:T(8,128)(2,1)S(1)}, bf16[32,1,10,128]{3,2,1,0:T(8,128)(2,1)S(1)}, u32[]{:S(2)}, u32[]{:S(2)}) collective-permute-start(bf16[32,1,10,128]{3,2,1,0:T(8,128)(2,1)S(1)} %get-tuple-element.60), channel_id=1, source_target_pairs={{32,0},{36,4},{40,8},{44,12},{48,16},{52,20},{56,24},{60,28},{64,3... | collective-permute-start | bytes 245768 | tf_op jit(solution)/shard_map/ppermute | solution.py:23
  34.0 40.0 %copy-start.3 = (pred[10,10,10,128]{3,2,1,0:T(8,128)(4,1)}, pred[10,10,10,128]{3,2,1,0:T(8,128)(4,1)S(1)}, u32[]{:S(2)}) copy-start(pred[10,10,10,128]{3,2,1,0:T(8,128)(4,1)S(1)} %get-tuple-element.52) | copy-start | bytes 384004
  48.1 4.3 %collective-permute-start.4 = (bf16[32,8,1,128]{3,2,1,0:T(2,128)(2,1)S(1)}, bf16[32,8,1,128]{3,2,1,0:T(2,128)(2,1)S(1)}, u32[]{:S(2)}, u32[]{:S(2)}) collective-permute-start(bf16[32,8,1,128]{3,2,1,0:T(2,128)(2,1)S(1)} %get-tuple-element.65), channel_id=1, source_target_pairs={{0,4},{4,8},{8,12},{12,16},{16,20},{20,24},{24,28},{28,32},{32,36}... | collective-permute-start | bytes 196616 | tf_op jit(solution)/shard_map/ppermute | solution.py:23
  49.4 6.8 %collective-permute-start.5 = (bf16[32,8,1,128]{3,2,1,0:T(2,128)(2,1)S(1)}, bf16[32,8,1,128]{3,2,1,0:T(2,128)(2,1)S(1)}, u32[]{:S(2)}, u32[]{:S(2)}) collective-permute-start(bf16[32,8,1,128]{3,2,1,0:T(2,128)(2,1)S(1)} %get-tuple-element.66), channel_id=1, source_target_pairs={{4,0},{8,4},{12,8},{16,12},{20,16},{24,20},{28,24},{32,28},{36,32}... | collective-permute-start | bytes 196616 | tf_op jit(solution)/shard_map/ppermute | solution.py:23
  56.5 11.2 %collective-permute-start.6 = (bf16[32,1,10,128]{3,2,1,0:T(8,128)(2,1)S(1)}, bf16[32,1,10,128]{3,2,1,0:T(8,128)(2,1)S(1)}, u32[]{:S(2)}, u32[]{:S(2)}) collective-permute-start(bf16[32,1,10,128]{3,2,1,0:T(8,128)(2,1)S(1)} %get-tuple-element.57), channel_id=1, source_target_pairs={{0,32},{4,36},{8,40},{12,44},{16,48},{20,52},{24,56},{28,60},{32,6... | collective-permute-start | bytes 245768 | tf_op jit(solution)/shard_map/ppermute | solution.py:23
  65.8 8.2 %collective-permute-start.7 = (bf16[32,1,10,128]{3,2,1,0:T(8,128)(2,1)S(1)}, bf16[32,1,10,128]{3,2,1,0:T(8,128)(2,1)S(1)}, u32[]{:S(2)}, u32[]{:S(2)}) collective-permute-start(bf16[32,1,10,128]{3,2,1,0:T(8,128)(2,1)S(1)} %get-tuple-element.58), channel_id=1, source_target_pairs={{32,0},{36,4},{40,8},{44,12},{48,16},{52,20},{56,24},{60,28},{64,3... | collective-permute-start | bytes 245768 | tf_op jit(solution)/shard_map/ppermute | solution.py:23
  76.3 11.5 %copy-start.1 = (bf16[1,8,8,8,3456]{4,3,2,1,0:T(8,128)(2,1)}, bf16[1,8,8,8,3456]{4,3,2,1,0:T(8,128)(2,1)S(1)}, u32[]{:S(2)}) copy-start(bf16[1,8,8,8,3456]{4,3,2,1,0:T(8,128)(2,1)S(1)} %constant_dynamic-update-slice_fusion.27) | copy-start | bytes 10616836
  88.1 4.3 %collective-permute-start.8 = (bf16[32,8,1,128]{3,2,1,0:T(2,128)(2,1)S(1)}, bf16[32,8,1,128]{3,2,1,0:T(2,128)(2,1)S(1)}, u32[]{:S(2)}, u32[]{:S(2)}) collective-permute-start(bf16[32,8,1,128]{3,2,1,0:T(2,128)(2,1)S(1)} %get-tuple-element.63), channel_id=1, source_target_pairs={{0,4},{4,8},{8,12},{12,16},{16,20},{20,24},{24,28},{28,32},{32,36}... | collective-permute-start | bytes 196616 | tf_op jit(solution)/shard_map/ppermute | solution.py:23
  89.4 6.8 %collective-permute-start.9 = (bf16[32,8,1,128]{3,2,1,0:T(2,128)(2,1)S(1)}, bf16[32,8,1,128]{3,2,1,0:T(2,128)(2,1)S(1)}, u32[]{:S(2)}, u32[]{:S(2)}) collective-permute-start(bf16[32,8,1,128]{3,2,1,0:T(2,128)(2,1)S(1)} %get-tuple-element.64), channel_id=1, source_target_pairs={{4,0},{8,4},{12,8},{16,12},{20,16},{24,20},{28,24},{32,28},{36,32}... | collective-permute-start | bytes 196616 | tf_op jit(solution)/shard_map/ppermute | solution.py:23
  97.2 15.9 %collective-permute-start.10 = (bf16[32,1,10,128]{3,2,1,0:T(8,128)(2,1)}, bf16[32,1,10,128]{3,2,1,0:T(8,128)(2,1)}, u32[]{:S(2)}, u32[]{:S(2)}) collective-permute-start(bf16[32,1,10,128]{3,2,1,0:T(8,128)(2,1)} %get-tuple-element.55), channel_id=1, source_target_pairs={{0,32},{4,36},{8,40},{12,44},{16,48},{20,52},{24,56},{28,60},{32,6... | collective-permute-start | bytes 245768 | tf_op jit(solution)/shard_map/ppermute | solution.py:23
  107.2 6.2 %collective-permute-start.11 = (bf16[32,1,10,128]{3,2,1,0:T(8,128)(2,1)}, bf16[32,1,10,128]{3,2,1,0:T(8,128)(2,1)}, u32[]{:S(2)}, u32[]{:S(2)}) collective-permute-start(bf16[32,1,10,128]{3,2,1,0:T(8,128)(2,1)} %get-tuple-element.56), channel_id=1, source_target_pairs={{32,0},{36,4},{40,8},{44,12},{48,16},{52,20},{56,24},{60,28},{64,3... | collective-permute-start | bytes 245768 | tf_op jit(solution)/shard_map/ppermute | solution.py:23
  116.7 12.6 %copy-start.2 = (bf16[1,8,8,8,3456]{4,3,2,1,0:T(8,128)(2,1)S(1)}, bf16[1,8,8,8,3456]{4,3,2,1,0:T(8,128)(2,1)}, u32[]{:S(2)}) copy-start(bf16[1,8,8,8,3456]{4,3,2,1,0:T(8,128)(2,1)} %copy-done.1) | copy-start | bytes 10616836
  116.7 12.6 %copy-start.11 = (f32[512,128]{1,0:T(8,128)S(1)}, f32[512,128]{1,0:T(8,128)}, u32[]{:S(2)}) copy-start(f32[512,128]{1,0:T(8,128)} %get-tuple-element.72) | copy-start | bytes 786436
  116.7 12.6 %copy-start.13 = (bf16[1,1,512,128]{3,2,1,0:T(8,128)(2,1)S(1)}, bf16[1,1,512,128]{3,2,1,0:T(8,128)(2,1)}, u32[]{:S(2)}) copy-start(bf16[1,1,512,128]{3,2,1,0:T(8,128)(2,1)} %param.7) | copy-start | bytes 393220
  128.0 4.4 %collective-permute-start.12 = (bf16[32,8,1,128]{3,2,1,0:T(2,128)(2,1)S(1)}, bf16[32,8,1,128]{3,2,1,0:T(2,128)(2,1)S(1)}, u32[]{:S(2)}, u32[]{:S(2)}) collective-permute-start(bf16[32,8,1,128]{3,2,1,0:T(2,128)(2,1)S(1)} %get-tuple-element.61), channel_id=1, source_target_pairs={{0,4},{4,8},{8,12},{12,16},{16,20},{20,24},{24,28},{28,32},{32,36}... | collective-permute-start | bytes 196616 | tf_op jit(solution)/shard_map/ppermute | solution.py:23
  131.1 6.8 %collective-permute-start.13 = (bf16[32,8,1,128]{3,2,1,0:T(2,128)(2,1)S(1)}, bf16[32,8,1,128]{3,2,1,0:T(2,128)(2,1)S(1)}, u32[]{:S(2)}, u32[]{:S(2)}) collective-permute-start(bf16[32,8,1,128]{3,2,1,0:T(2,128)(2,1)S(1)} %get-tuple-element.62), channel_id=1, source_target_pairs={{4,0},{8,4},{12,8},{16,12},{20,16},{24,20},{28,24},{32,28},{36,32}... | collective-permute-start | bytes 196616 | tf_op jit(solution)/shard_map/ppermute | solution.py:23
  138.2 58.0 %collective-permute-start.14 = (bf16[32,1,10,128]{3,2,1,0:T(8,128)(2,1)S(1)}, bf16[32,1,10,128]{3,2,1,0:T(8,128)(2,1)S(1)}, u32[]{:S(2)}, u32[]{:S(2)}) collective-permute-start(bf16[32,1,10,128]{3,2,1,0:T(8,128)(2,1)S(1)} %get-tuple-element.53), channel_id=1, source_target_pairs={{0,32},{4,36},{8,40},{12,44},{16,48},{20,52},{24,56},{28,60},{32,6... | collective-permute-start | bytes 245768 | tf_op jit(solution)/shard_map/ppermute | solution.py:23
  148.3 47.9 %collective-permute-start.15 = (bf16[32,1,10,128]{3,2,1,0:T(8,128)(2,1)S(1)}, bf16[32,1,10,128]{3,2,1,0:T(8,128)(2,1)S(1)}, u32[]{:S(2)}, u32[]{:S(2)}) collective-permute-start(bf16[32,1,10,128]{3,2,1,0:T(8,128)(2,1)S(1)} %get-tuple-element.54), channel_id=1, source_target_pairs={{32,0},{36,4},{40,8},{44,12},{48,16},{52,20},{56,24},{60,28},{64,3... | collective-permute-start | bytes 245768 | tf_op jit(solution)/shard_map/ppermute | solution.py:23
  150.8 45.5 %copy-start.4 = (pred[10,10,10,128]{3,2,1,0:T(8,128)(4,1)S(1)}, pred[10,10,10,128]{3,2,1,0:T(8,128)(4,1)}, u32[]{:S(2)}) copy-start(pred[10,10,10,128]{3,2,1,0:T(8,128)(4,1)} %copy-done.3) | copy-start | bytes 384004
  (9 other events, 24.7 us)

commit v2 on v1

v2 whole, which is shorter than its diff:
```python
import itertools

import jax
import jax.numpy as jnp
from jax import lax
from jax.experimental import pallas as pl
from jax.experimental.pallas import tpu as pltpu
from jax.sharding import PartitionSpec as P

MESH = pl.DeviceIdType.MESH
SLOPE_COEF = 0.7978845608028654
CUBIC_COEF = 0.044715
PLANE = 16
DEEP = 16
PIECE = 8
ROWS = 27 * 128
STEPS = [d for d in itertools.product((-1, 0, 1), repeat=3) if d != (0, 0, 0)]
F32 = jnp.float32
BF16 = jnp.bfloat16


def far_first(step, count):
    half = count // 2
    return half + (step + 1) // 2 * (1 - 2 * (step % 2))


def gelu_terms(values):
    inner = SLOPE_COEF * (values + CUBIC_COEF * values * values * values)
    tangent = jnp.tanh(inner)
    slope = 0.5 * (1.0 + tangent) + 0.5 * values * (1.0 - tangent * tangent) * SLOPE_COEF * (
        1.0 + 3.0 * CUBIC_COEF * values * values
    )
    return 0.5 * values * (1.0 + tangent), slope


class Spot:
    def __init__(self):
        self.space = lax.axis_index("space")
        self.depth = lax.axis_index("depth")
        self.deep = self.space // 8
        self.column = self.space % 8
        self.core = self.depth % 2
        self.x_lo = self.depth // 2
        self.plane = self.column * 2 + self.x_lo

    def plane_peer(self, rank):
        return (self.deep * 8 + rank // 2, rank % 2 * 2 + self.core)

    def deep_peer(self, rank):
        return (rank * 8 + self.column, self.depth)

    def column_peer(self, rank):
        return (self.space, rank)

    def tile_peer(self, step):
        z, x, y = step
        return ((self.deep + x + 16) % 16 * 8 + (self.column + y + 8) % 8, (self.depth + z + 4) % 4)


def greet(spot):
    barrier = pltpu.get_barrier_semaphore()

    def tell(peer):
        pl.semaphore_signal(barrier, inc=1, device_id=peer, device_id_type=MESH)

    @pl.loop(0, 15)
    def _(step):
        tell(spot.deep_peer((spot.deep + far_first(step, 16)) % 16))

    @pl.loop(0, 15)
    def _(step):
        tell(spot.plane_peer((spot.plane + step + 1) % 16))

    for step in STEPS:
        tell(spot.tile_peer(step))
    for step in range(1, 4):
        tell(spot.column_peer((spot.depth + step) % 4))
    pl.semaphore_wait(barrier, 30 + len(STEPS) + 3)


def send(source, target, send_sem, recv_sem, peer):
    return pltpu.make_async_remote_copy(
        src_ref=source, dst_ref=target, send_sem=send_sem, recv_sem=recv_sem, device_id=peer, device_id_type=MESH
    )


class Gather:
    def __init__(self, spot, refs):
        self.spot = spot
        self.tiles, self.sems = refs

    @staticmethod
    def scratch():
        return [pltpu.VMEM((4, 512, 128), BF16), pltpu.SemaphoreType.DMA((2, 4))]

    def copy(self, source, step):
        me = self.spot.depth
        rank = (me + step) % 4
        return send(source, self.tiles.at[me], self.sems.at[0, rank], self.sems.at[1, me], self.spot.column_peer(rank))

    def start(self, source):
        for step in (2, 3, 1):
            self.copy(source, step).start()

    def finish(self, source):
        me = self.spot.depth
        for step in (1, 2, 3):
            rank = (me + step) % 4
            send(source, self.tiles.at[rank], self.sems.at[0, rank], self.sems.at[1, rank],
                 self.spot.column_peer(rank)).wait_recv()

    def drain(self, source):
        for step in (1, 2, 3):
            self.copy(source, step).wait_send()

    def pick(self, weights, rows):
        total = weights[0] * self.tiles[0, rows, :].astype(F32)
        for rank in range(1, 4):
            total = total + weights[rank] * self.tiles[rank, rows, :].astype(F32)
        return total


def side(step):
    return 0 if step == 1 else 1


def last(step):
    return 7 if step == 1 else 0


class Halo:
    def __init__(self, spot, refs):
        self.spot = spot
        (self.tile, self.y_face, self.xy_edge, self.in_z, self.in_x, self.in_y, self.in_zx, self.in_zy, self.in_xy,
         self.in_zxy, self.sems) = refs

    @staticmethod
    def scratch():
        shapes = [(8, 8), (2, 8), (2, 2), (2, 8), (2, 8), (2, 8), (2, 2), (2, 2), (2, 2), (2, 2, 2)]
        return [pltpu.VMEM((*shape, 8, 128), BF16) for shape in shapes] + [pltpu.SemaphoreType.DMA((2, 26))]

    def ends(self, step):
        z, x, y = step
        if y == 0:
            if x == 0:
                return self.tile.at[last(z)], self.in_z.at[side(z)]
            if z == 0:
                return self.tile.at[:, last(x)], self.in_x.at[side(x)]
            return self.tile.at[last(z), last(x)], self.in_zx.at[side(z), side(x)]
        if x == 0:
            if z == 0:
                return self.y_face.at[side(y)], self.in_y.at[side(y)]
            return self.y_face.at[side(y), last(z)], self.in_zy.at[side(z), side(y)]
        if z == 0:
            return self.xy_edge.at[side(x), side(y)], self.in_xy.at[side(x), side(y)]
        return self.xy_edge.at[side(x), side(y)], self.in_zxy.at[side(z), side(x), side(y)]

    def copies(self):
        order = sorted(range(26), key=lambda n: -abs(STEPS[n][2]) * 10 - sum(abs(d) for d in STEPS[n]))
        for n in order:
            source, target = self.ends(STEPS[n])
            yield send(source, target, self.sems.at[0, n], self.sems.at[1, n], self.spot.tile_peer(STEPS[n]))

    def put(self, centre, values):
        rounded = values.astype(BF16).reshape(8, 8, 8, 128)
        self.tile[...] = rounded
        centre[1:9, 1:9] = rounded.astype(F32)
        flat = centre.reshape(800, 128)
        for z in range(8):
            for y in range(2):
                first = ((z + 1) * 10 + 1) * 8 + 7 - 7 * y
                self.y_face[y, z] = flat[pl.ds(first, 8, stride=8), :].astype(BF16)
        for x in range(2):
            for y in range(2):
                first = (10 + 8 - 7 * x) * 8 + 7 - 7 * y
                self.xy_edge[x, y] = flat[pl.ds(first, 8, stride=80), :].astype(BF16)

    def start(self):
        for copy in self.copies():
            copy.start()

    def finish(self, centre, lines, masks, cols):
        for copy in self.copies():
            copy.wait_recv()
        on_z, on_x, on_y = masks
        ends = (0, 9)
        for s in range(2):
            centre[ends[s], 1:9] = self.in_z[s].astype(F32) * on_z[s]
            centre[1:9, ends[s]] = self.in_x[s].astype(F32) * on_x[s]
            lines[s, 1:9, 0:8] = self.in_y[s].astype(F32) * on_y[s]
            for r in range(2):
                centre[ends[s], ends[r]] = self.in_zx[s, r].astype(F32) * (on_z[s] * on_x[r])
                lines[r, ends[s], 0:8] = self.in_zy[s, r].astype(F32) * (on_z[s] * on_y[r])
                rows = self.in_xy[s, r].astype(F32) * (on_x[s] * on_y[r])
                for z in range(8):
                    lines[r, 1 + z, 8 + s : 9 + s] = rows[z : z + 1]
                for q in range(2):
                    rows = self.in_zxy[s, r, q].astype(F32) * (on_z[s] * on_x[r] * on_y[q])
                    row = 7 - 7 * s
                    lines[q, ends[s], 8 + r : 9 + r] = rows[row : row + 1]
        row_id = lax.broadcasted_iota(jnp.int32, (8, 128), 0)

        @pl.loop(0, 10)
        def _(z):
            runs = ([], [], [])
            for x in range(10):
                place = 8 if x == 0 else 9 if x == 9 else x - 1
                middle = centre[z, x]
                low = jnp.broadcast_to(lines[0, z, place : place + 1], (8, 128))
                high = jnp.broadcast_to(lines[1, z, place : place + 1], (8, 128))
                runs[0].append(jnp.where(row_id == 0, low, pltpu.roll(middle, 1, 0)))
                runs[1].append(middle)
                runs[2].append(jnp.where(row_id == 7, high, pltpu.roll(middle, 7, 0)))
            for x in range(3):
                for y in range(3):
                    block = jnp.concatenate(runs[y][x : x + 8], axis=0).astype(BF16)
                    cols[z, :, (3 * x + y) * 128 : (3 * x + y + 1) * 128] = block

    def drain(self):
        for copy in self.copies():
            copy.wait_send()


class Scatter:
    def __init__(self, spot, refs):
        self.spot = spot
        (self.halves, self.partner, self.merged, self.plane_in, self.deep_out, self.deep_in, self.pieces, self.sems,
         self.plane_sems, self.deep_sems, self.piece_sems) = refs

    @staticmethod
    def scratch():
        return [
            pltpu.VMEM((2, PLANE, DEEP, PIECE, 128), BF16),
            pltpu.VMEM((PLANE, DEEP, PIECE, 128), BF16),
            pltpu.VMEM((PLANE, DEEP, PIECE, 128), BF16),
            pltpu.VMEM((PLANE, DEEP, PIECE, 128), BF16),
            pltpu.VMEM((DEEP, PIECE, 128), F32),
            pltpu.VMEM((DEEP, PIECE, 128), F32),
            pltpu.VMEM((4, PIECE, 128), F32),
            pltpu.SemaphoreType.DMA((2,)),
            pltpu.SemaphoreType.DMA((2, 16)),
            pltpu.SemaphoreType.DMA((2, 16)),
            pltpu.SemaphoreType.DMA((2, 4)),
        ]

    def cut(self, grad_ref):

        @pl.loop(0, DEEP)
        def _(z):
            rows = grad_ref[pl.ds(pl.multiple_of(z * 216, 8), 216), :]
            rows = jnp.concatenate([rows, jnp.zeros((8, 128), F32)], axis=0)
            for column in range(8):
                for part in range(4):
                    first = column * 27 + part * 8
                    self.halves[part % 2, column * 2 + part // 2, z] = rows[first : first + 8].astype(BF16)

    def pair_copy(self):
        spot = self.spot
        other = 1 - spot.core
        return send(self.halves.at[other], self.partner, self.sems.at[0], self.sems.at[1],
                    spot.column_peer(spot.x_lo * 2 + other))

    def merge(self):
        self.pair_copy().wait_recv()
        core = self.spot.core

        @pl.loop(0, PLANE)
        def _(rank):
            both = self.halves[core, rank].astype(F32) + self.partner[rank].astype(F32)
            self.merged[rank] = both.astype(BF16)

        @pl.loop(1, PLANE)
        def _(step):
            self.plane_copy(step).start()

    def plane_copy(self, step):
        me = self.spot.plane
        rank = (me + step) % PLANE
        return send(self.merged.at[rank], self.plane_in.at[me], self.plane_sems.at[0, rank], self.plane_sems.at[1, me],
                    self.spot.plane_peer(rank))

    def plane_arrival(self, step):
        me = self.spot.plane
        rank = (me + step) % PLANE
        return send(self.merged.at[rank], self.plane_in.at[rank], self.plane_sems.at[0, rank],
                    self.plane_sems.at[1, rank], self.spot.plane_peer(rank))

    def plane_finish(self):
        me = self.spot.plane
        self.plane_in[me] = self.merged[me]

        @pl.loop(1, PLANE)
        def _(step):
            self.plane_arrival(step).wait_recv()

        @pl.loop(0, DEEP)
        def _(z):
            total = jnp.zeros((PIECE, 128), F32)
            for rank in range(PLANE):
                total = total + self.plane_in[rank, z].astype(F32)
            self.deep_out[z] = total

        @pl.loop(0, DEEP - 1)
        def _(step):
            self.deep_copy(step).start()

    def deep_copy(self, step):
        me = self.spot.deep
        rank = (me + far_first(step, DEEP)) % DEEP
        return send(self.deep_out.at[rank], self.deep_in.at[me], self.deep_sems.at[0, rank], self.deep_sems.at[1, me],
                    self.spot.deep_peer(rank))

    def deep_arrival(self, step):
        me = self.spot.deep
        rank = (me + far_first(step, DEEP)) % DEEP
        return send(self.deep_out.at[rank], self.deep_in.at[rank], self.deep_sems.at[0, rank],
                    self.deep_sems.at[1, rank], self.spot.deep_peer(rank))

    def deep_finish(self):
        me = self.spot.deep
        self.deep_in[me] = self.deep_out[me]

        @pl.loop(0, DEEP - 1)
        def _(step):
            self.deep_arrival(step).wait_recv()

        total = jnp.zeros((PIECE, 128), F32)
        for rank in range(DEEP):
            total = total + self.deep_in[rank]
        self.pieces[self.spot.depth] = total * (1.0 / 512)
        for step in range(1, 4):
            self.piece_copy(step).start()

    def piece_copy(self, step):
        me = self.spot.depth
        rank = (me + step) % 4
        return send(self.pieces.at[me], self.pieces.at[me], self.piece_sems.at[0, rank], self.piece_sems.at[1, me],
                    self.spot.column_peer(rank))

    def piece_arrival(self, step):
        me = self.spot.depth
        rank = (me + step) % 4
        return send(self.pieces.at[rank], self.pieces.at[rank], self.piece_sems.at[0, rank],
                    self.piece_sems.at[1, rank], self.spot.column_peer(rank))

    def piece_finish(self, out_ref):
        for step in range(1, 4):
            self.piece_arrival(step).wait_recv()
        for rank in range(4):
            out_ref[rank] = self.pieces[rank]

    def drain(self):
        self.pair_copy().wait_send()

        @pl.loop(1, PLANE)
        def _(step):
            self.plane_copy(step).wait_send()

        @pl.loop(0, DEEP - 1)
        def _(step):
            self.deep_copy(step).wait_send()

        for step in range(1, 4):
            self.piece_copy(step).wait_send()


def convolve(cols, kernel_ref):
    total = None
    for z in range(3):
        rows = cols[z : z + 8].reshape(512, 9 * 128)
        term = jnp.dot(rows, kernel_ref[z], preferred_element_type=F32)
        total = term if total is None else total + term
    return total


def turn(kernel_ref, turned):
    @pl.loop(0, 27)
    def _(k):
        turned[26 - k] = kernel_ref[k].T


def kernel_gradient(cols, delta, grad_ref):
    for z in range(3):
        rows = cols[z : z + 8].reshape(512, 9 * 128)
        grad_ref[z * 1152 : (z + 1) * 1152] = lax.dot_general(
            rows, delta, (((0,), (0,)), ((), ())), preferred_element_type=F32
        )


def body(features, cotangent, first_hbm, second_hbm, slot_tile, slot_used, grad_out, first_out, second_out, *scratch):
    spot = Spot()
    scratch = list(scratch)

    def take(kind):
        count = len(kind.scratch())
        refs = scratch[:count]
        del scratch[:count]
        return kind(spot, refs)

    source_in, upstream_in, back_in = (take(Gather) for _ in range(3))
    halo_one, halo_two, halo_three, halo_four = (take(Halo) for _ in range(4))
    scatter_one, scatter_two = (take(Scatter) for _ in range(2))
    (first_kernel, second_kernel, first_turned, second_turned, centre, lines, source_cols, act_cols, delta_cols, grad_one,
     grad_two, upstream, slope_one, result, load_sems) = scratch

    loads = [
        pltpu.make_async_copy(first_hbm, first_kernel, load_sems.at[0]),
        pltpu.make_async_copy(second_hbm, second_kernel, load_sems.at[1]),
    ]
    for load in loads:
        load.start()
    greet(spot)
    source_in.start(features)
    upstream_in.start(cotangent)

    me = spot.depth
    source_in.tiles[me] = features[...]
    upstream_in.tiles[me] = cotangent[...]
    weights = [jnp.where(slot_tile[0, j] == me, 1.0, 0.0) * slot_used[0, j].astype(F32) for j in range(4)]
    alive = weights[0] + weights[1] + weights[2] + weights[3]
    own_tile = slot_tile[0, me]
    own_used = slot_used[0, me].astype(F32)

    def mask(condition):
        return jnp.where(condition, 1.0, 0.0)

    masks = (
        (mask(spot.depth > 0), mask(spot.depth < 3)),
        (mask(spot.deep > 0), mask(spot.deep < 15)),
        (mask(spot.column > 0), mask(spot.column < 7)),
    )
    for load in loads:
        load.wait()
    turn(second_kernel, second_turned)
    turn(first_kernel, first_turned)
    first_taps = first_kernel.reshape(3, 1152, 128)
    second_taps = second_kernel.reshape(3, 1152, 128)
    first_back = first_turned.reshape(3, 1152, 128)
    second_back = second_turned.reshape(3, 1152, 128)

    source_in.finish(features)
    halo_one.put(centre, source_in.pick(weights, slice(None)))
    halo_one.start()
    upstream_in.finish(cotangent)
    upstream[...] = upstream_in.pick(weights, slice(None))
    halo_one.finish(centre, lines, masks, source_cols)
    act, slope = gelu_terms(convolve(source_cols, first_taps))
    slope_one[...] = slope * alive
    halo_two.put(centre, act * alive)
    halo_two.start()
    halo_two.finish(centre, lines, masks, act_cols)
    _, slope = gelu_terms(convolve(act_cols, second_taps))
    halo_three.put(centre, upstream[...] * slope * alive)
    halo_three.start()
    kernel_gradient(act_cols, halo_three.tile[...].reshape(512, 128), grad_two)
    scatter_two.cut(grad_two)
    scatter_two.pair_copy().start()
    halo_three.finish(centre, lines, masks, delta_cols)
    halo_four.put(centre, convolve(delta_cols, second_back) * slope_one[...])
    halo_four.start()
    kernel_gradient(source_cols, halo_four.tile[...].reshape(512, 128), grad_one)
    scatter_one.cut(grad_one)
    scatter_one.pair_copy().start()
    scatter_two.merge()
    scatter_one.merge()
    halo_four.finish(centre, lines, masks, delta_cols)
    result[...] = convolve(delta_cols, first_back).astype(BF16)
    back_in.start(result)
    back_in.tiles[me] = result[...]
    scatter_two.plane_finish()
    scatter_one.plane_finish()
    back_in.finish(result)
    picks = [mask(own_tile == t) * own_used for t in range(4)]
    grad_out[...] = back_in.pick(picks, slice(None)).astype(BF16)
    scatter_two.deep_finish()
    scatter_one.deep_finish()
    scatter_two.piece_finish(second_out)
    scatter_one.piece_finish(first_out)
    source_in.drain(features)
    upstream_in.drain(cotangent)
    back_in.drain(result)
    for halo in (halo_one, halo_two, halo_three, halo_four):
        halo.drain()
    scatter_two.drain()
    scatter_one.drain()


def fused(features, cotangent, first_kernel, second_kernel, slot_tile, slot_used):
    whole = pl.BlockSpec(memory_space=pltpu.VMEM)
    left = pl.BlockSpec(memory_space=pl.ANY)
    small = pl.BlockSpec(memory_space=pltpu.SMEM)
    piece = jax.ShapeDtypeStruct((4, PIECE, 128), F32)
    cols = pltpu.VMEM((10, 64, 9 * 128), BF16)
    kernel = pltpu.VMEM((27, 128, 128), BF16)
    scratch = Gather.scratch() * 3 + Halo.scratch() * 4 + Scatter.scratch() * 2
    scratch += [kernel] * 4 + [pltpu.VMEM((10, 10, 8, 128), F32), pltpu.VMEM((2, 10, 16, 128), F32)] + [cols] * 3
    scratch += [pltpu.VMEM((ROWS, 128), F32)] * 2 + [pltpu.VMEM((512, 128), F32)] * 2
    scratch += [pltpu.VMEM((512, 128), BF16), pltpu.SemaphoreType.DMA((2,))]
    return pl.pallas_call(
        body,
        out_shape=(jax.ShapeDtypeStruct((512, 128), BF16), piece, piece),
        in_specs=[whole, whole, left, left, small, small],
        out_specs=(whole, whole, whole),
        scratch_shapes=scratch,
        compiler_params=pltpu.CompilerParams(collective_id=0, has_side_effects=True, vmem_limit_bytes=56 << 20),
    )(features, cotangent, first_kernel, second_kernel, slot_tile, slot_used)


def on_device(features, cotangent, first_kernel, second_kernel, slot_tile, slot_used):
    grad, first_sum, second_sum = fused(
        features.reshape(512, 128), cotangent.reshape(512, 128), first_kernel, second_kernel, slot_tile, slot_used
    )
    own_share = ROWS // 4

    def share(total):
        return lax.dynamic_slice_in_dim(total.reshape(-1), lax.axis_index("depth") * own_share, own_share, 0)

    return (grad.reshape(features.shape), share(first_sum), share(second_sum))


def solution(mesh):
    tiles = P("space", "depth", None, None)
    slots = P("space", None)
    share = P(("space", "depth"))
    return jax.shard_map(
        on_device,
        mesh=mesh,
        in_specs=(tiles, tiles, P(), P(), slots, slots),
        out_specs=(tiles, share, share),
        check_vma=False,
    )
```

time: 201 us -> 85.8 us (0.43)
  starting transfers between devices: 48.1 us -> 0 us
  blocking collectives: 39.6 us -> 0 us
  Pallas kernels: 44.1 us -> 80.7 us
  waiting for transfers between devices: 30.2 us -> 0 us
  matrix products: 13.9 us -> 0 us
  local copies, waits for them, and re-layouts: 13.3 us -> 4.3 us
  other arithmetic: 7.82 us -> 0 us
  between operations: 3.73 us -> 0.65 us
    ppermute x16 -> x0, starting transfers between devices: 48.1 us -> none  [from_behind(): return lax.ppermute(block, axis, route)]
    all_gather x4 -> x0, blocking collectives: 39.6 us -> none  [dense_column(): lax.all_gather(tile_rows, 'depth', axis=0, tiled=True)]
    pallas_call x1, Pallas kernels: 44.1 us -> 80.7 us  [fused(): pl.pallas_call(body, out_shape=(jax.ShapeDtypeStruct((512, 128), BF16), p...]
    ppermute x16 -> x0, waiting for transfers between devices: 30.2 us -> none  [from_behind(): return lax.ppermute(block, axis, route)]
    dot_general x10 -> x0, matrix products: 13.9 us -> none  [the longest x2 2.92 us: tile_sum(): lax.dot_general(columns, delta, (((0,), (0,)), ((), ())), preferred_eleme...]
    unnamed x140 -> x1, local copies, waits for them, and re-layouts: 10.8 us -> 1.57 us
    gather x4 -> x0, other arithmetic: 3.08 us -> none  [one_window(): return lax.dynamic_slice_in_dim(padded, z_index * TE, TE + 2, 0)]
  transfers between devices with their start and end apart: 16 -> 0, of which waited for: 11 -> 0; matrix products, arithmetic and copies ran while one was open for 5% -> 0% of each run, Pallas kernels for 22% -> 0%
where the time goes in v2:
time: 85.8 us; the launch traced here: 85.6 us
  Pallas kernels  80.7 us (94%)
  local copies, waits for them, and re-layouts  4.3 us (5%)
    pallas_call x1, Pallas kernels, fused(): pl.pallas_call(body, out_shape=(jax.ShapeDtypeStruct((512, 128), BF16), p...  80.7 us
    dynamic_slice x2, local copies, waits for them, and re-layouts, share(): lax.dynamic_slice_in_dim(total.reshape(-1), lax.axis_index('depth') * own...  2.73 us

profile of v2, /device:TPU:1, one launch (start us, length us, event | category | flops | bytes accessed | tf_op | source)
XLA Modules:
  0.0 85.6 jit_solution(9759873543266555691)
XLA Ops:
  0.6 80.7 %shard_map.85 = (bf16[512,128]{1,0:T(8,128)(2,1)}, f32[4,8,128]{2,1,0:T(8,128)}, f32[4,8,128]{2,1,0:T(8,128)}) custom-call(bf16[512,128]{1,0:T(8,128)(2,1)} %bitcast.5, bf16[512,128]{1,0:T(8,128)(2,1)} %bitcast.6, bf16[27,128,128]{2,1,0:T(8,128)(2,1)} %first_hbm.1, bf16[27,128,128]{2,1,0:T(8,128)(2,1)} %second_hbm.1, s32[1,4]{1,0:T(1,128)} %slot_tile.1, ...), custom_call_target="tpu_custom_call" | custom-call | tf_op jit(solution)/shard_map/pallas_call | solution.py:499
  81.3 1.4 %dynamic_slice.6 = f32[864]{0:T(1024)} dynamic-slice(f32[4096]{0:T(1024)} %bitcast.9, s32[]{:T(128)S(6)} %select_n.4), dynamic_slice_sizes={864} | dynamic-slice | bytes 6916 | tf_op jit(solution)/shard_map/dynamic_slice | solution.py:516
  82.7 1.4 %dynamic_slice.7 = f32[864]{0:T(1024)} dynamic-slice(f32[4096]{0:T(1024)} %bitcast.8, s32[]{:T(128)S(6)} %select_n.4), dynamic_slice_sizes={864} | dynamic-slice | bytes 6916 | tf_op jit(solution)/shard_map/dynamic_slice | solution.py:516
  84.0 1.6 %copy.10 = bf16[1,1,512,128]{3,2,1,0:T(8,128)(2,1)} copy(bf16[1,1,512,128]{3,2,1,0:T(8,128)(2,1)} %bitcast.7) | data formatting | bytes 262144

commit v3 on v2

--- a/solution.py
+++ b/solution.py
@@ -63,19 +63,33 @@
     def tell(peer):
         pl.semaphore_signal(barrier, inc=1, device_id=peer, device_id_type=MESH)
 
-    @pl.loop(0, 15)
-    def _(step):
-        tell(spot.deep_peer((spot.deep + far_first(step, 16)) % 16))
-
-    @pl.loop(0, 15)
-    def _(step):
-        tell(spot.plane_peer((spot.plane + step + 1) % 16))
-
     for step in STEPS:
         tell(spot.tile_peer(step))
     for step in range(1, 4):
         tell(spot.column_peer((spot.depth + step) % 4))
-    pl.semaphore_wait(barrier, 30 + len(STEPS) + 3)
+    pl.semaphore_wait(barrier, len(STEPS) + 3)
+
+
+class News:
+    def __init__(self, spot, refs):
+        self.spot = spot
+        (self.sem,) = refs
+
+    @staticmethod
+    def scratch():
+        return [pltpu.SemaphoreType.REGULAR((3,))]
+
+    def peers(self, level):
+        reach = 2**level
+        steps = [(0, reach, 0), (0, -reach, 0), (0, 0, reach)] + ([(0, 0, -reach)] if level < 2 else [])
+        return [self.spot.tile_peer(step) for step in steps]
+
+    def tell(self, level):
+        for peer in self.peers(level):
+            pl.semaphore_signal(self.sem.at[level], inc=1, device_id=peer, device_id_type=MESH)
+
+    def hear(self, level):
+        pl.semaphore_wait(self.sem.at[level], len(self.peers(level)))
 
 
 def send(source, target, send_sem, recv_sem, peer):
@@ -88,30 +102,42 @@
     def __init__(self, spot, refs):
         self.spot = spot
         self.tiles, self.sems = refs
+        self.me = spot.depth
+        self.pair = spot.x_lo * 2 + 1 - spot.core
+        self.across = (1 - spot.x_lo) * 2 + spot.core
+        self.diagonal = (1 - spot.x_lo) * 2 + 1 - spot.core
 
     @staticmethod
     def scratch():
-        return [pltpu.VMEM((4, 512, 128), BF16), pltpu.SemaphoreType.DMA((2, 4))]
-
-    def copy(self, source, step):
-        me = self.spot.depth
-        rank = (me + step) % 4
-        return send(source, self.tiles.at[me], self.sems.at[0, rank], self.sems.at[1, me], self.spot.column_peer(rank))
-
-    def start(self, source):
-        for step in (2, 3, 1):
-            self.copy(source, step).start()
-
-    def finish(self, source):
-        me = self.spot.depth
-        for step in (1, 2, 3):
-            rank = (me + step) % 4
-            send(source, self.tiles.at[rank], self.sems.at[0, rank], self.sems.at[1, rank],
-                 self.spot.column_peer(rank)).wait_recv()
-
-    def drain(self, source):
-        for step in (1, 2, 3):
-            self.copy(source, step).wait_send()
+        return [pltpu.VMEM((4, 512, 128), BF16), pltpu.SemaphoreType.DMA((2, 3))]
+
+    def copy(self, way):
+        tile = self.across if way == 2 else self.me
+        peer = self.across if way == 0 else self.pair
+        return send(self.tiles.at[tile], self.tiles.at[tile], self.sems.at[0, way], self.sems.at[1, way],
+                    self.spot.column_peer(peer))
+
+    def arrival(self, way):
+        tile = (self.across, self.pair, self.diagonal)[way]
+        peer = self.across if way == 0 else self.pair
+        return send(self.tiles.at[tile], self.tiles.at[tile], self.sems.at[0, way], self.sems.at[1, way],
+                    self.spot.column_peer(peer))
+
+    def start(self):
+        self.copy(0).start()
+        self.copy(1).start()
+
+    def relay(self):
+        self.arrival(0).wait_recv()
+        self.copy(2).start()
+
+    def finish(self):
+        self.arrival(1).wait_recv()
+        self.arrival(2).wait_recv()
+
+    def drain(self):
+        for way in range(3):
+            self.copy(way).wait_send()
 
     def pick(self, weights, rows):
         total = weights[0] * self.tiles[0, rows, :].astype(F32)
@@ -224,8 +250,8 @@
 class Scatter:
     def __init__(self, spot, refs):
         self.spot = spot
-        (self.halves, self.partner, self.merged, self.plane_in, self.deep_out, self.deep_in, self.pieces, self.sems,
-         self.plane_sems, self.deep_sems, self.piece_sems) = refs
+        (self.halves, self.partner, self.merged, self.plane_in, self.deep_out, self.deep_in, self.sems,
+         self.plane_sems, self.deep_sems) = refs
 
     @staticmethod
     def scratch():
@@ -234,13 +260,11 @@
             pltpu.VMEM((PLANE, DEEP, PIECE, 128), BF16),
             pltpu.VMEM((PLANE, DEEP, PIECE, 128), BF16),
             pltpu.VMEM((PLANE, DEEP, PIECE, 128), BF16),
-            pltpu.VMEM((DEEP, PIECE, 128), F32),
-            pltpu.VMEM((DEEP, PIECE, 128), F32),
-            pltpu.VMEM((4, PIECE, 128), F32),
+            pltpu.VMEM((DEEP, PIECE, 128), BF16),
+            pltpu.VMEM((DEEP, PIECE, 128), BF16),
             pltpu.SemaphoreType.DMA((2,)),
             pltpu.SemaphoreType.DMA((2, 16)),
             pltpu.SemaphoreType.DMA((2, 16)),
-            pltpu.SemaphoreType.DMA((2, 4)),
         ]
 
     def cut(self, grad_ref):
@@ -251,7 +275,7 @@
             rows = jnp.concatenate([rows, jnp.zeros((8, 128), F32)], axis=0)
             for column in range(8):
                 for part in range(4):
-                    first = column * 27 + part * 8
+                    first = column * 27 + part * 27 // 4
                     self.halves[part % 2, column * 2 + part // 2, z] = rows[first : first + 8].astype(BF16)
 
     def pair_copy(self):
@@ -298,7 +322,7 @@
             total = jnp.zeros((PIECE, 128), F32)
             for rank in range(PLANE):
                 total = total + self.plane_in[rank, z].astype(F32)
-            self.deep_out[z] = total
+            self.deep_out[z] = total.astype(BF16)
 
         @pl.loop(0, DEEP - 1)
         def _(step):
@@ -316,7 +340,7 @@
         return send(self.deep_out.at[rank], self.deep_in.at[rank], self.deep_sems.at[0, rank],
                     self.deep_sems.at[1, rank], self.spot.deep_peer(rank))
 
-    def deep_finish(self):
+    def deep_finish(self, out_ref):
         me = self.spot.deep
         self.deep_in[me] = self.deep_out[me]
 
@@ -326,28 +350,16 @@
 
         total = jnp.zeros((PIECE, 128), F32)
         for rank in range(DEEP):
-            total = total + self.deep_in[rank]
-        self.pieces[self.spot.depth] = total * (1.0 / 512)
-        for step in range(1, 4):
-            self.piece_copy(step).start()
-
-    def piece_copy(self, step):
-        me = self.spot.depth
-        rank = (me + step) % 4
-        return send(self.pieces.at[me], self.pieces.at[me], self.piece_sems.at[0, rank], self.piece_sems.at[1, me],
-                    self.spot.column_peer(rank))
-
-    def piece_arrival(self, step):
-        me = self.spot.depth
-        rank = (me + step) % 4
-        return send(self.pieces.at[rank], self.pieces.at[rank], self.piece_sems.at[0, rank],
-                    self.piece_sems.at[1, rank], self.spot.column_peer(rank))
-
-    def piece_finish(self, out_ref):
-        for step in range(1, 4):
-            self.piece_arrival(step).wait_recv()
-        for rank in range(4):
-            out_ref[rank] = self.pieces[rank]
+            total = total + self.deep_in[rank].astype(F32)
+        total = total * (1.0 / 512)
+        lane = lax.broadcasted_iota(jnp.int32, (PIECE, 128), 1)
+        share = total
+        for depth in range(1, 4):
+            ahead = 128 - 32 * depth
+            turned = pltpu.roll(total, 128 - ahead, 1)
+            moved = jnp.where(lane < 128 - ahead, turned, pltpu.roll(turned, 7, 0))
+            share = jnp.where(self.spot.depth == depth, moved, share)
+        out_ref[...] = share
 
     def drain(self):
         self.pair_copy().wait_send()
@@ -359,9 +371,6 @@
         @pl.loop(0, DEEP - 1)
         def _(step):
             self.deep_copy(step).wait_send()
-
-        for step in range(1, 4):
-            self.piece_copy(step).wait_send()
 
 
 def convolve(cols, kernel_ref):
@@ -400,22 +409,24 @@
     source_in, upstream_in, back_in = (take(Gather) for _ in range(3))
     halo_one, halo_two, halo_three, halo_four = (take(Halo) for _ in range(4))
     scatter_one, scatter_two = (take(Scatter) for _ in range(2))
+    news = take(News)
     (first_kernel, second_kernel, first_turned, second_turned, centre, lines, source_cols, act_cols, delta_cols, grad_one,
-     grad_two, upstream, slope_one, result, load_sems) = scratch
-
+     grad_two, upstream, slope_one, load_sems) = scratch
+
+    me = spot.depth
     loads = [
-        pltpu.make_async_copy(first_hbm, first_kernel, load_sems.at[0]),
-        pltpu.make_async_copy(second_hbm, second_kernel, load_sems.at[1]),
+        pltpu.make_async_copy(features, source_in.tiles.at[me], load_sems.at[0]),
+        pltpu.make_async_copy(cotangent, upstream_in.tiles.at[me], load_sems.at[1]),
+        pltpu.make_async_copy(second_hbm, second_kernel, load_sems.at[2]),
+        pltpu.make_async_copy(first_hbm, first_kernel, load_sems.at[3]),
     ]
     for load in loads:
         load.start()
     greet(spot)
-    source_in.start(features)
-    upstream_in.start(cotangent)
-
-    me = spot.depth
-    source_in.tiles[me] = features[...]
-    upstream_in.tiles[me] = cotangent[...]
+    loads[0].wait()
+    source_in.start()
+    news.tell(0)
+
     weights = [jnp.where(slot_tile[0, j] == me, 1.0, 0.0) * slot_used[0, j].astype(F32) for j in range(4)]
     alive = weights[0] + weights[1] + weights[2] + weights[3]
     own_tile = slot_tile[0, me]
@@ -429,25 +440,32 @@
         (mask(spot.deep > 0), mask(spot.deep < 15)),
         (mask(spot.column > 0), mask(spot.column < 7)),
     )
-    for load in loads:
+    for load in loads[1:]:
         load.wait()
     turn(second_kernel, second_turned)
-    turn(first_kernel, first_turned)
     first_taps = first_kernel.reshape(3, 1152, 128)
     second_taps = second_kernel.reshape(3, 1152, 128)
     first_back = first_turned.reshape(3, 1152, 128)
     second_back = second_turned.reshape(3, 1152, 128)
 
-    source_in.finish(features)
+    source_in.relay()
+    source_in.finish()
     halo_one.put(centre, source_in.pick(weights, slice(None)))
     halo_one.start()
-    upstream_in.finish(cotangent)
-    upstream[...] = upstream_in.pick(weights, slice(None))
+    upstream_in.start()
+    turn(first_kernel, first_turned)
+    news.hear(0)
+    news.tell(1)
     halo_one.finish(centre, lines, masks, source_cols)
     act, slope = gelu_terms(convolve(source_cols, first_taps))
     slope_one[...] = slope * alive
     halo_two.put(centre, act * alive)
     halo_two.start()
+    upstream_in.relay()
+    news.hear(1)
+    news.tell(2)
+    upstream_in.finish()
+    upstream[...] = upstream_in.pick(weights, slice(None))
     halo_two.finish(centre, lines, masks, act_cols)
     _, slope = gelu_terms(convolve(act_cols, second_taps))
     halo_three.put(centre, upstream[...] * slope * alive)
@@ -455,51 +473,57 @@
     kernel_gradient(act_cols, halo_three.tile[...].reshape(512, 128), grad_two)
     scatter_two.cut(grad_two)
     scatter_two.pair_copy().start()
+    news.hear(2)
+    scatter_two.merge()
     halo_three.finish(centre, lines, masks, delta_cols)
     halo_four.put(centre, convolve(delta_cols, second_back) * slope_one[...])
     halo_four.start()
     kernel_gradient(source_cols, halo_four.tile[...].reshape(512, 128), grad_one)
     scatter_one.cut(grad_one)
     scatter_one.pair_copy().start()
-    scatter_two.merge()
     scatter_one.merge()
     halo_four.finish(centre, lines, masks, delta_cols)
-    result[...] = convolve(delta_cols, first_back).astype(BF16)
-    back_in.start(result)
-    back_in.tiles[me] = result[...]
+    back_in.tiles[me] = convolve(delta_cols, first_back).astype(BF16)
+    back_in.start()
     scatter_two.plane_finish()
     scatter_one.plane_finish()
-    back_in.finish(result)
+    scatter_two.deep_finish(second_out)
+    back_in.relay()
+    back_in.finish()
     picks = [mask(own_tile == t) * own_used for t in range(4)]
     grad_out[...] = back_in.pick(picks, slice(None)).astype(BF16)
-    scatter_two.deep_finish()
-    scatter_one.deep_finish()
-    scatter_two.piece_finish(second_out)
-    scatter_one.piece_finish(first_out)
-    source_in.drain(features)
-    upstream_in.drain(cotangent)
-    back_in.drain(result)
+    scatter_one.deep_finish(first_out)
+    for gather in (source_in, upstream_in, back_in):
+        gather.drain()
     for halo in (halo_one, halo_two, halo_three, halo_four):
         halo.drain()
     scatter_two.drain()
     scatter_one.drain()
 
 
+def hand_out(grad, first, second, grad_out, first_out, second_out):
+    grad_out[...] = grad[...]
+    for source, target in ((first, first_out), (second, second_out)):
+        for row in range(6):
+            target[row * 128 : (row + 1) * 128] = source[row]
+        target[768:864] = source[6, :96]
+
+
 def fused(features, cotangent, first_kernel, second_kernel, slot_tile, slot_used):
     whole = pl.BlockSpec(memory_space=pltpu.VMEM)
     left = pl.BlockSpec(memory_space=pl.ANY)
     small = pl.BlockSpec(memory_space=pltpu.SMEM)
-    piece = jax.ShapeDtypeStruct((4, PIECE, 128), F32)
+    piece = jax.ShapeDtypeStruct((PIECE, 128), F32)
     cols = pltpu.VMEM((10, 64, 9 * 128), BF16)
     kernel = pltpu.VMEM((27, 128, 128), BF16)
-    scratch = Gather.scratch() * 3 + Halo.scratch() * 4 + Scatter.scratch() * 2
+    scratch = Gather.scratch() * 3 + Halo.scratch() * 4 + Scatter.scratch() * 2 + News.scratch()
     scratch += [kernel] * 4 + [pltpu.VMEM((10, 10, 8, 128), F32), pltpu.VMEM((2, 10, 16, 128), F32)] + [cols] * 3
     scratch += [pltpu.VMEM((ROWS, 128), F32)] * 2 + [pltpu.VMEM((512, 128), F32)] * 2
-    scratch += [pltpu.VMEM((512, 128), BF16), pltpu.SemaphoreType.DMA((2,))]
+    scratch += [pltpu.SemaphoreType.DMA((4,))]
     return pl.pallas_call(
         body,
         out_shape=(jax.ShapeDtypeStruct((512, 128), BF16), piece, piece),
-        in_specs=[whole, whole, left, left, small, small],
+        in_specs=[left, left, left, left, small, small],
         out_specs=(whole, whole, whole),
         scratch_shapes=scratch,
         compiler_params=pltpu.CompilerParams(collective_id=0, has_side_effects=True, vmem_limit_bytes=56 << 20),
@@ -507,15 +531,18 @@
 
 
 def on_device(features, cotangent, first_kernel, second_kernel, slot_tile, slot_used):
-    grad, first_sum, second_sum = fused(
+    sums = fused(
         features.reshape(512, 128), cotangent.reshape(512, 128), first_kernel, second_kernel, slot_tile, slot_used
     )
-    own_share = ROWS // 4
-
-    def share(total):
-        return lax.dynamic_slice_in_dim(total.reshape(-1), lax.axis_index("depth") * own_share, own_share, 0)
-
-    return (grad.reshape(features.shape), share(first_sum), share(second_sum))
+    share = jax.ShapeDtypeStruct((ROWS // 4,), F32)
+    whole = pl.BlockSpec(memory_space=pltpu.VMEM)
+    grad, first, second = pl.pallas_call(
+        hand_out,
+        out_shape=(jax.ShapeDtypeStruct((512, 128), BF16), share, share),
+        in_specs=[whole] * 3,
+        out_specs=(whole,) * 3,
+    )(*sums)
+    return (grad.reshape(features.shape), first, second)
 
 
 def solution(mesh):

time: 85.8 us -> 70.8 us (0.83)
  Pallas kernels: 80.7 us -> 70.1 us
  local copies, waits for them, and re-layouts: 4.3 us -> 0 us
    pallas_call x1, Pallas kernels: 80.7 us -> 68.5 us  [fused(): pl.pallas_call(body, out_shape=(jax.ShapeDtypeStruct((512, 128), BF16), p...]
    dynamic_slice x2 -> x0, local copies, waits for them, and re-layouts: 2.73 us -> none  [share(): lax.dynamic_slice_in_dim(total.reshape(-1), lax.axis_index('depth') * own...]
    pallas_call x0 -> x1, Pallas kernels: none -> 1.58 us  [on_device(): pl.pallas_call(hand_out, out_shape=(jax.ShapeDtypeStruct((512, 128), BF16...]
    unnamed x1 -> x0, local copies, waits for them, and re-layouts: 1.57 us -> none
where the time goes in v3:
time: 70.8 us; the launch traced here: 70.7 us
  Pallas kernels  70.1 us (99%)
    pallas_call x1, Pallas kernels, fused(): pl.pallas_call(body, out_shape=(jax.ShapeDtypeStruct((512, 128), BF16), p...  68.5 us
    pallas_call x1, Pallas kernels, on_device(): pl.pallas_call(hand_out, out_shape=(jax.ShapeDtypeStruct((512, 128), BF16...  1.58 us

profile of v3, /device:TPU:1, one launch (start us, length us, event | category | flops | bytes accessed | tf_op | source)
XLA Modules:
  0.0 70.7 jit_solution(15179215399088247982)
XLA Ops:
  0.6 68.5 %shard_map.85 = (bf16[512,128]{1,0:T(8,128)(2,1)}, f32[8,128]{1,0:T(8,128)}, f32[8,128]{1,0:T(8,128)}) custom-call(bf16[512,128]{1,0:T(8,128)(2,1)} %bitcast.3, bf16[512,128]{1,0:T(8,128)(2,1)} %bitcast.4, bf16[27,128,128]{2,1,0:T(8,128)(2,1)} %first_hbm.1, bf16[27,128,128]{2,1,0:T(8,128)(2,1)} %second_hbm.1, s32[1,4]{1,0:T(1,128)} %slot_tile.1, ...), custom_call_target="tpu_custom_call" | custom-call | tf_op jit(solution)/shard_map/pallas_call | solution.py:523
  69.1 1.6 %shard_map.86 = (bf16[512,128]{1,0:T(8,128)(2,1)}, f32[864]{0:T(1024)}, f32[864]{0:T(1024)}) custom-call(bf16[512,128]{1,0:T(8,128)(2,1)} %get-tuple-element.9.grad, f32[8,128]{1,0:T(8,128)} %get-tuple-element.10.first, f32[8,128]{1,0:T(8,128)} %get-tuple-element.11.second), custom_call_target="tpu_custom_call" | custom-call | tf_op jit(solution)/shard_map/pallas_call | solution.py:539

commit v4 on v3

v4 whole, which is shorter than its diff:
```python
import itertools

import jax
import jax.numpy as jnp
from jax import lax
from jax.experimental import pallas as pl
from jax.experimental.pallas import tpu as pltpu
from jax.sharding import PartitionSpec as P

MESH = pl.DeviceIdType.MESH
SLOPE_COEF = 0.7978845608028654
CUBIC_COEF = 0.044715
PLANE = 16
DEEP = 16
PIECE = 8
ROWS = 27 * 128
STEPS = [d for d in itertools.product((-1, 0, 1), repeat=3) if d != (0, 0, 0)]
PLANE_STEPS = sorted(
    [(x, y) for x in range(4) for y in range(4) if (x, y) != (0, 0)],
    key=lambda step: -min(step[0], 4 - step[0]) - min(step[1], 4 - step[1]),
)
DEEP_STEPS = sorted(range(1, DEEP), key=lambda step: -min(step, DEEP - step))
PARTS = ((0, 5), (5, 10), (10, DEEP))
F32 = jnp.float32
BF16 = jnp.bfloat16


def gelu_terms(values):
    inner = SLOPE_COEF * (values + CUBIC_COEF * values * values * values)
    tangent = jnp.tanh(inner)
    slope = 0.5 * (1.0 + tangent) + 0.5 * values * (1.0 - tangent * tangent) * SLOPE_COEF * (
        1.0 + 3.0 * CUBIC_COEF * values * values
    )
    return 0.5 * values * (1.0 + tangent), slope


class Spot:
    def __init__(self):
        self.space = lax.axis_index("space")
        self.depth = lax.axis_index("depth")
        self.deep = self.space // 8
        self.column = self.space % 8
        self.core = self.depth % 2
        self.x_lo = self.depth // 2
        self.plane = self.column * 2 + self.x_lo

    def plane_step(self, x, y):
        far_x = lax.rem(self.column // 4 * 2 + self.x_lo + x, 4)
        far_y = lax.rem(self.column % 4 + y, 4)
        high, low = lax.div(far_x, 2), lax.rem(far_x, 2)
        column = high * 4 + far_y
        return column * 2 + low, (self.deep * 8 + column, low * 2 + self.core)

    def deep_peer(self, rank):
        return (rank * 8 + self.column, self.depth)

    def column_peer(self, rank):
        return (self.space, rank)

    def tile_peer(self, step):
        z, x, y = step
        return (lax.rem(self.deep + x + 16, 16) * 8 + lax.rem(self.column + y + 8, 8), lax.rem(self.depth + z + 4, 4))


def greet(spot):
    barrier = pltpu.get_barrier_semaphore()

    def tell(peer):
        pl.semaphore_signal(barrier, inc=1, device_id=peer, device_id_type=MESH)

    for step in STEPS:
        tell(spot.tile_peer(step))
    for step in range(1, 4):
        tell(spot.column_peer((spot.depth + step) % 4))
    pl.semaphore_wait(barrier, len(STEPS) + 3)


class News:
    def __init__(self, spot, refs):
        self.spot = spot
        (self.sem,) = refs

    @staticmethod
    def scratch():
        return [pltpu.SemaphoreType.REGULAR((3,))]

    def peers(self, level):
        reach = 2**level
        steps = [(0, reach, 0), (0, -reach, 0), (0, 0, reach)] + ([(0, 0, -reach)] if level < 2 else [])
        return [self.spot.tile_peer(step) for step in steps]

    def tell(self, level):
        for peer in self.peers(level):
            pl.semaphore_signal(self.sem.at[level], inc=1, device_id=peer, device_id_type=MESH)

    def hear(self, level):
        pl.semaphore_wait(self.sem.at[level], len(self.peers(level)))


def send(source, target, send_sem, recv_sem, peer):
    return pltpu.make_async_remote_copy(
        src_ref=source, dst_ref=target, send_sem=send_sem, recv_sem=recv_sem, device_id=peer, device_id_type=MESH
    )


class Gather:
    def __init__(self, spot, refs):
        self.spot = spot
        self.tiles, self.sems = refs
        self.me = spot.depth
        self.pair = spot.x_lo * 2 + 1 - spot.core
        self.across = (1 - spot.x_lo) * 2 + spot.core
        self.diagonal = (1 - spot.x_lo) * 2 + 1 - spot.core

    @staticmethod
    def scratch():
        return [pltpu.VMEM((4, 512, 128), BF16), pltpu.SemaphoreType.DMA((2, 4))]

    def part(self, tile, half, way, peer):
        rows = self.tiles.at[tile] if half is None else self.tiles.at[tile, half * 256 : (half + 1) * 256]
        return send(rows, rows, self.sems.at[0, way], self.sems.at[1, way], self.spot.column_peer(peer))

    def start(self):
        for half in range(2):
            self.part(self.me, half, half, self.across).start()
        self.part(self.me, None, 2, self.pair).start()

    def relay(self):
        for half in range(2):
            self.part(self.across, half, half, self.across).wait_recv()
            self.part(self.across, half, 3, self.pair).start()

    def finish(self):
        self.part(self.pair, None, 2, self.pair).wait_recv()
        self.part(self.diagonal, None, 3, self.pair).wait_recv()

    def drain(self):
        for half in range(2):
            self.part(self.me, half, half, self.across).wait_send()
        self.part(self.me, None, 2, self.pair).wait_send()
        self.part(self.across, None, 3, self.pair).wait_send()

    def pick(self, weights, rows):
        total = weights[0] * self.tiles[0, rows, :].astype(F32)
        for rank in range(1, 4):
            total = total + weights[rank] * self.tiles[rank, rows, :].astype(F32)
        return total


def side(step):
    return 0 if step == 1 else 1


def last(step):
    return 7 if step == 1 else 0


class Halo:
    def __init__(self, spot, refs):
        self.spot = spot
        self.tile, self.y_face, self.xy_edge, self.inbox, self.sems = refs

    @staticmethod
    def scratch():
        shapes = [(8, 8), (2, 8), (2, 2), (68,)]
        return [pltpu.VMEM((*shape, 8, 128), BF16) for shape in shapes] + [pltpu.SemaphoreType.DMA((2,))]

    def face(self, axis, s):
        return self.inbox.at[axis * 16 + s * 8 : axis * 16 + s * 8 + 8]

    def edge(self, plane, s, r):
        return self.inbox.at[48 + plane * 4 + 2 * s + r]

    def corner(self, s, r, q):
        return self.inbox.at[60 + 4 * s + 2 * r + q]

    def ends(self, step):
        z, x, y = step
        if y == 0:
            if x == 0:
                return self.tile.at[last(z)], self.face(0, side(z))
            if z == 0:
                return self.tile.at[:, last(x)], self.face(1, side(x))
            return self.tile.at[last(z), last(x)], self.edge(0, side(z), side(x))
        if x == 0:
            if z == 0:
                return self.y_face.at[side(y)], self.face(2, side(y))
            return self.y_face.at[side(y), last(z)], self.edge(1, side(z), side(y))
        if z == 0:
            return self.xy_edge.at[side(x), side(y)], self.edge(2, side(x), side(y))
        return self.xy_edge.at[side(x), side(y)], self.corner(side(z), side(x), side(y))

    def whole(self):
        return send(self.inbox, self.inbox, self.sems.at[0], self.sems.at[1], self.spot.tile_peer((0, 0, 1)))

    def put(self, centre, values):
        rounded = values.astype(BF16).reshape(8, 8, 8, 128)
        self.tile[...] = rounded
        centre[1:9, 1:9] = rounded.astype(F32)
        flat = centre.reshape(800, 128)
        for z in range(8):
            for y in range(2):
                first = ((z + 1) * 10 + 1) * 8 + 7 - 7 * y
                self.y_face[y, z] = flat[pl.ds(first, 8, stride=8), :].astype(BF16)
        for x in range(2):
            for y in range(2):
                first = (10 + 8 - 7 * x) * 8 + 7 - 7 * y
                self.xy_edge[x, y] = flat[pl.ds(first, 8, stride=80), :].astype(BF16)

    def start(self):
        order = sorted(STEPS, key=lambda step: -abs(step[2]) * 10 - sum(abs(d) for d in step))
        for step in order:
            source, target = self.ends(step)
            send(source, target, self.sems.at[0], self.sems.at[1], self.spot.tile_peer(step)).start()

    def finish(self, centre, lines, masks, cols):
        self.whole().wait_recv()
        on_z, on_x, on_y = masks
        ends = (0, 9)
        for s in range(2):
            centre[ends[s], 1:9] = self.face(0, s)[...].astype(F32) * on_z[s]
            centre[1:9, ends[s]] = self.face(1, s)[...].astype(F32) * on_x[s]
            lines[s, 1:9, 0:8] = self.face(2, s)[...].astype(F32) * on_y[s]
            for r in range(2):
                centre[ends[s], ends[r]] = self.edge(0, s, r)[...].astype(F32) * (on_z[s] * on_x[r])
                lines[r, ends[s], 0:8] = self.edge(1, s, r)[...].astype(F32) * (on_z[s] * on_y[r])
                rows = self.edge(2, s, r)[...].astype(F32) * (on_x[s] * on_y[r])
                for z in range(8):
                    lines[r, 1 + z, 8 + s : 9 + s] = rows[z : z + 1]
                for q in range(2):
                    rows = self.corner(s, r, q)[...].astype(F32) * (on_z[s] * on_x[r] * on_y[q])
                    row = 7 - 7 * s
                    lines[q, ends[s], 8 + r : 9 + r] = rows[row : row + 1]
        row_id = lax.broadcasted_iota(jnp.int32, (8, 128), 0)

        @pl.loop(0, 10)
        def _(z):
            runs = ([], [], [])
            for x in range(10):
                place = 8 if x == 0 else 9 if x == 9 else x - 1
                middle = centre[z, x]
                low = jnp.broadcast_to(lines[0, z, place : place + 1], (8, 128))
                high = jnp.broadcast_to(lines[1, z, place : place + 1], (8, 128))
                runs[0].append(jnp.where(row_id == 0, low, pltpu.roll(middle, 1, 0)))
                runs[1].append(middle)
                runs[2].append(jnp.where(row_id == 7, high, pltpu.roll(middle, 7, 0)))
            for x in range(3):
                for y in range(3):
                    block = jnp.concatenate(runs[y][x : x + 8], axis=0).astype(BF16)
                    cols[z, :, (3 * x + y) * 128 : (3 * x + y + 1) * 128] = block

    def drain(self):
        self.whole().wait_send()


class Scatter:
    def __init__(self, spot, refs):
        self.spot = spot
        (self.halves, self.partner, self.merged, self.plane_in, self.deep_out, self.deep_in, self.grad, self.pair_sems,
         self.plane_sems, self.deep_sems) = refs

    @staticmethod
    def scratch():
        return [
            pltpu.VMEM((2, PLANE, DEEP, PIECE, 128), BF16),
            pltpu.VMEM((PLANE, DEEP, PIECE, 128), BF16),
            pltpu.VMEM((PLANE, DEEP, PIECE, 128), BF16),
            pltpu.VMEM((PLANE, DEEP, PIECE, 128), BF16),
            pltpu.VMEM((DEEP, PIECE, 128), BF16),
            pltpu.VMEM((DEEP, PIECE, 128), BF16),
            pltpu.VMEM((ROWS, 128), F32),
            pltpu.SemaphoreType.DMA((2, len(PARTS))),
            pltpu.SemaphoreType.DMA((2,)),
            pltpu.SemaphoreType.DMA((2,)),
        ]

    def produce(self, cols, delta):
        for part, (first, end) in enumerate(PARTS):
            rows = cols[part : part + 8].reshape(512, 9 * 128)
            self.grad[part * 1152 : (part + 1) * 1152] = lax.dot_general(
                rows, delta, (((0,), (0,)), ((), ())), preferred_element_type=F32
            )
            self.cut(first, end)
            self.pair_copy(part).start()

    def cut(self, first_z, end_z):

        @pl.loop(first_z, end_z)
        def _(z):
            rows = self.grad[pl.ds(pl.multiple_of(z * 216, 8), 216), :]
            rows = jnp.concatenate([rows, jnp.zeros((8, 128), F32)], axis=0)
            for column in range(8):
                for part in range(4):
                    first = column * 27 + part * 27 // 4
                    self.halves[part % 2, column * 2 + part // 2, z] = rows[first : first + 8].astype(BF16)

    def pair_copy(self, part):
        spot = self.spot
        other = 1 - spot.core
        first, end = PARTS[part]
        return send(self.halves.at[other, :, first:end], self.partner.at[:, first:end], self.pair_sems.at[0, part],
                    self.pair_sems.at[1, part], spot.column_peer(spot.x_lo * 2 + other))

    def merge(self, together):
        core = self.spot.core
        for part, (first, end) in enumerate(PARTS):
            self.pair_copy(part).wait_recv()
            for rank in range(PLANE):
                own = self.halves[core, rank, first:end].astype(F32)
                both = own + self.partner[rank, first:end].astype(F32)
                self.merged[rank, first:end] = both.astype(BF16)
            if not together:
                self.plane_start(first, end)
        if together:
            self.plane_start(0, DEEP)

    def plane_start(self, first, end):
        spot = self.spot
        for x, y in PLANE_STEPS:
            rank, peer = spot.plane_step(x, y)
            send(self.merged.at[rank, first:end], self.plane_in.at[spot.plane, first:end], self.plane_sems.at[0],
                 self.plane_sems.at[1], peer).start()

    def plane_whole(self):
        return send(self.merged.at[0 : PLANE - 1], self.plane_in.at[0 : PLANE - 1], self.plane_sems.at[0],
                    self.plane_sems.at[1], self.spot.plane_step(1, 0)[1])

    def plane_finish(self):
        me = self.spot.plane
        self.plane_in[me] = self.merged[me]
        self.plane_whole().wait_recv()

        @pl.loop(0, DEEP)
        def _(z):
            total = jnp.zeros((PIECE, 128), F32)
            for rank in range(PLANE):
                total = total + self.plane_in[rank, z].astype(F32)
            self.deep_out[z] = total.astype(BF16)

        for step in DEEP_STEPS:
            rank = lax.rem(self.spot.deep + step, DEEP)
            send(self.deep_out.at[rank], self.deep_in.at[self.spot.deep], self.deep_sems.at[0], self.deep_sems.at[1],
                 self.spot.deep_peer(rank)).start()

    def deep_whole(self):
        return send(self.deep_out.at[0 : DEEP - 1], self.deep_in.at[0 : DEEP - 1], self.deep_sems.at[0],
                    self.deep_sems.at[1], self.spot.deep_peer(lax.rem(self.spot.deep + 1, DEEP)))

    def deep_finish(self, out_ref):
        me = self.spot.deep
        self.deep_in[me] = self.deep_out[me]
        self.deep_whole().wait_recv()

        total = jnp.zeros((PIECE, 128), F32)
        for rank in range(DEEP):
            total = total + self.deep_in[rank].astype(F32)
        total = total * (1.0 / 512)
        lane = lax.broadcasted_iota(jnp.int32, (PIECE, 128), 1)
        share = total
        for depth in range(1, 4):
            ahead = 128 - 32 * depth
            turned = pltpu.roll(total, 128 - ahead, 1)
            moved = jnp.where(lane < 128 - ahead, turned, pltpu.roll(turned, 7, 0))
            share = jnp.where(self.spot.depth == depth, moved, share)
        out_ref[...] = share

    def drain(self):
        for part in range(len(PARTS)):
            self.pair_copy(part).wait_send()
        self.plane_whole().wait_send()
        self.deep_whole().wait_send()


def convolve(cols, kernel_ref):
    total = None
    for z in range(3):
        rows = cols[z : z + 8].reshape(512, 9 * 128)
        term = jnp.dot(rows, kernel_ref[z], preferred_element_type=F32)
        total = term if total is None else total + term
    return total


def turn(kernel_ref, turned):
    @pl.loop(0, 27)
    def _(k):
        turned[26 - k] = kernel_ref[k].T


def body(features, cotangent, first_hbm, second_hbm, tile_hbm, used_hbm, grad_out, first_out, second_out, *scratch):
    spot = Spot()
    scratch = list(scratch)

    def take(kind):
        count = len(kind.scratch())
        refs = scratch[:count]
        del scratch[:count]
        return kind(spot, refs)

    source_in, upstream_in, back_in = (take(Gather) for _ in range(3))
    halo_one, halo_two, halo_three, halo_four = (take(Halo) for _ in range(4))
    scatter_one, scatter_two = (take(Scatter) for _ in range(2))
    news = take(News)
    (first_kernel, second_kernel, first_turned, second_turned, centre, lines, source_cols, act_cols, delta_cols, upstream,
     slope_one, slot_tile, slot_used, load_sems) = scratch

    me = spot.depth
    loads = [
        pltpu.make_async_copy(features, source_in.tiles.at[me], load_sems.at[0]),
        pltpu.make_async_copy(tile_hbm, slot_tile, load_sems.at[4]),
        pltpu.make_async_copy(used_hbm, slot_used, load_sems.at[5]),
        pltpu.make_async_copy(cotangent, upstream_in.tiles.at[me], load_sems.at[1]),
        pltpu.make_async_copy(second_hbm, second_kernel, load_sems.at[2]),
        pltpu.make_async_copy(first_hbm, first_kernel, load_sems.at[3]),
    ]
    for load in loads:
        load.start()
    greet(spot)
    loads[0].wait()
    source_in.start()
    news.tell(0)
    for load in loads[1:3]:
        load.wait()

    weights = [jnp.where(slot_tile[0, j] == me, 1.0, 0.0) * slot_used[0, j].astype(F32) for j in range(4)]
    alive = weights[0] + weights[1] + weights[2] + weights[3]
    own_tile = slot_tile[0, me]
    own_used = slot_used[0, me].astype(F32)

    def mask(condition):
        return jnp.where(condition, 1.0, 0.0)

    masks = (
        (mask(spot.depth > 0), mask(spot.depth < 3)),
        (mask(spot.deep > 0), mask(spot.deep < 15)),
        (mask(spot.column > 0), mask(spot.column < 7)),
    )
    first_taps = first_kernel.reshape(3, 1152, 128)
    second_taps = second_kernel.reshape(3, 1152, 128)
    first_back = first_turned.reshape(3, 1152, 128)
    second_back = second_turned.reshape(3, 1152, 128)

    source_in.relay()
    source_in.finish()
    halo_one.put(centre, source_in.pick(weights, slice(None)))
    halo_one.start()
    for load in loads[3:]:
        load.wait()
    upstream_in.start()
    turn(first_kernel, first_turned)
    news.hear(0)
    news.tell(1)
    halo_one.finish(centre, lines, masks, source_cols)
    act, slope = gelu_terms(convolve(source_cols, first_taps))
    slope_one[...] = slope * alive
    halo_two.put(centre, act * alive)
    halo_two.start()
    upstream_in.relay()
    news.hear(1)
    news.tell(2)
    turn(second_kernel, second_turned)
    upstream_in.finish()
    upstream[...] = upstream_in.pick(weights, slice(None))
    halo_two.finish(centre, lines, masks, act_cols)
    _, slope = gelu_terms(convolve(act_cols, second_taps))
    halo_three.put(centre, upstream[...] * slope * alive)
    halo_three.start()
    scatter_two.produce(act_cols, halo_three.tile[...].reshape(512, 128))
    news.hear(2)
    halo_three.finish(centre, lines, masks, delta_cols)
    scatter_two.merge(together=True)
    halo_four.put(centre, convolve(delta_cols, second_back) * slope_one[...])
    halo_four.start()
    scatter_one.produce(source_cols, halo_four.tile[...].reshape(512, 128))
    scatter_one.merge(together=False)
    halo_four.finish(centre, lines, masks, delta_cols)
    back_in.tiles[me] = convolve(delta_cols, first_back).astype(BF16)
    back_in.start()
    scatter_two.plane_finish()
    scatter_one.plane_finish()
    scatter_two.deep_finish(second_out)
    back_in.relay()
    back_in.finish()
    picks = [mask(own_tile == t) * own_used for t in range(4)]
    grad_out[...] = back_in.pick(picks, slice(None)).astype(BF16)
    scatter_one.deep_finish(first_out)
    for gather in (source_in, upstream_in, back_in):
        gather.drain()
    for halo in (halo_one, halo_two, halo_three, halo_four):
        halo.drain()
    scatter_two.drain()
    scatter_one.drain()


def hand_out(grad, first, second, grad_out, first_out, second_out):
    grad_out[...] = grad[...]
    for source, target in ((first, first_out), (second, second_out)):
        for row in range(6):
            target[row * 128 : (row + 1) * 128] = source[row]
        target[768:864] = source[6, :96]


def fused(features, cotangent, first_kernel, second_kernel, slot_tile, slot_used):
    whole = pl.BlockSpec(memory_space=pltpu.VMEM)
    left = pl.BlockSpec(memory_space=pl.ANY)
    piece = pltpu.VMEM((PIECE, 128), F32)
    cols = pltpu.VMEM((10, 64, 9 * 128), BF16)
    kernel = pltpu.VMEM((27, 128, 128), BF16)
    scratch = Gather.scratch() * 3 + Halo.scratch() * 4 + Scatter.scratch() * 2 + News.scratch()
    scratch += [kernel] * 4 + [pltpu.VMEM((10, 10, 8, 128), F32), pltpu.VMEM((2, 10, 16, 128), F32)] + [cols] * 3
    scratch += [pltpu.VMEM((512, 128), F32)] * 2 + [pltpu.SMEM((1, 4), jnp.int32)] * 2
    scratch += [pltpu.SemaphoreType.DMA((6,))]
    return pl.pallas_call(
        body,
        out_shape=(pltpu.VMEM((512, 128), BF16), piece, piece),
        in_specs=[left] * 6,
        out_specs=(whole, whole, whole),
        scratch_shapes=scratch,
        compiler_params=pltpu.CompilerParams(collective_id=0, has_side_effects=True, vmem_limit_bytes=56 << 20),
    )(features, cotangent, first_kernel, second_kernel, slot_tile, slot_used)


def on_device(features, cotangent, first_kernel, second_kernel, slot_tile, slot_used):
    sums = fused(
        features.reshape(512, 128), cotangent.reshape(512, 128), first_kernel, second_kernel, slot_tile, slot_used
    )
    share = jax.ShapeDtypeStruct((ROWS // 4,), F32)
    whole = pl.BlockSpec(memory_space=pltpu.VMEM)
    grad, first, second = pl.pallas_call(
        hand_out,
        out_shape=(jax.ShapeDtypeStruct((512, 128), BF16), share, share),
        in_specs=[whole] * 3,
        out_specs=(whole,) * 3,
    )(*(pltpu.with_memory_space_constraint(value, pltpu.VMEM) for value in sums))
    return (grad.reshape(features.shape), first, second)


def solution(mesh):
    tiles = P("space", "depth", None, None)
    slots = P("space", None)
    share = P(("space", "depth"))
    return jax.shard_map(
        on_device,
        mesh=mesh,
        in_specs=(tiles, tiles, P(), P(), slots, slots),
        out_specs=(tiles, share, share),
        check_vma=False,
    )
```

time: 70.8 us -> 65.9 us (0.931)
  Pallas kernels: 70.1 us -> 64.9 us
    pallas_call x1, Pallas kernels: 68.5 us -> 64.3 us  [fused(): pl.pallas_call(body, out_shape=(pltpu.VMEM((512, 128), BF16), piece, piec...]
    pallas_call x1, Pallas kernels: 1.58 us -> 0.68 us  [on_device(): pl.pallas_call(hand_out, out_shape=(jax.ShapeDtypeStruct((512, 128), BF16...]
where the time goes in v4:
time: 65.9 us; the launch traced here: 65.6 us
  Pallas kernels  64.9 us (98%)
    pallas_call x1, Pallas kernels, fused(): pl.pallas_call(body, out_shape=(pltpu.VMEM((512, 128), BF16), piece, piec...  64.3 us

profile of v4, /device:TPU:1, one launch (start us, length us, event | category | flops | bytes accessed | tf_op | source)
XLA Modules:
  0.0 65.6 jit_solution(1443564942380504999)
XLA Ops:
  0.6 64.3 %shard_map.85 = (bf16[512,128]{1,0:T(8,128)(2,1)S(1)}, f32[8,128]{1,0:T(8,128)S(1)}, f32[8,128]{1,0:T(8,128)S(1)}) custom-call(bf16[512,128]{1,0:T(8,128)(2,1)} %bitcast.3, bf16[512,128]{1,0:T(8,128)(2,1)} %bitcast.4, bf16[27,128,128]{2,1,0:T(8,128)(2,1)} %first_hbm.1, bf16[27,128,128]{2,1,0:T(8,128)(2,1)} %second_hbm.1, s32[1,4]{1,0:T(1,128)} %tile_hbm.1, ...), custom_call_target="tpu_custom_call" | custom-call | tf_op jit(solution)/shard_map/pallas_call | solution.py:512
  64.9 0.7 %shard_map.86 = (bf16[512,128]{1,0:T(8,128)(2,1)}, f32[864]{0:T(1024)}, f32[864]{0:T(1024)}) custom-call(bf16[512,128]{1,0:T(8,128)(2,1)S(1)} %get-tuple-element.9.grad, f32[8,128]{1,0:T(8,128)S(1)} %get-tuple-element.10.first, f32[8,128]{1,0:T(8,128)S(1)} %get-tuple-element.11.second), custom_call_target="tpu_custom_call" | custom-call | tf_op jit(solution)/shard_map/pallas_call | solution.py:528

commit v5 on v4

--- a/solution.py
+++ b/solution.py
@@ -19,7 +19,7 @@
     [(x, y) for x in range(4) for y in range(4) if (x, y) != (0, 0)],
     key=lambda step: -min(step[0], 4 - step[0]) - min(step[1], 4 - step[1]),
 )
-DEEP_STEPS = sorted(range(1, DEEP), key=lambda step: -min(step, DEEP - step))
+DEEP_STEPS = (8, 7, 9, 6, 10, 5, 11, 4, 12, 3, 13, 2, 14, 1, 15)
 PARTS = ((0, 5), (5, 10), (10, DEEP))
 F32 = jnp.float32
 BF16 = jnp.bfloat16
@@ -270,7 +270,7 @@
             pltpu.VMEM((DEEP, PIECE, 128), BF16),
             pltpu.VMEM((ROWS, 128), F32),
             pltpu.SemaphoreType.DMA((2, len(PARTS))),
-            pltpu.SemaphoreType.DMA((2,)),
+            pltpu.SemaphoreType.DMA((2, len(PARTS))),
             pltpu.SemaphoreType.DMA((2,)),
         ]
 
@@ -283,16 +283,20 @@
             self.cut(first, end)
             self.pair_copy(part).start()
 
+    def place(self, z):
+        return z
+
     def cut(self, first_z, end_z):
 
         @pl.loop(first_z, end_z)
         def _(z):
+            place = self.place(z)
             rows = self.grad[pl.ds(pl.multiple_of(z * 216, 8), 216), :]
             rows = jnp.concatenate([rows, jnp.zeros((8, 128), F32)], axis=0)
             for column in range(8):
                 for part in range(4):
                     first = column * 27 + part * 27 // 4
-                    self.halves[part % 2, column * 2 + part // 2, z] = rows[first : first + 8].astype(BF16)
+                    self.halves[part % 2, column * 2 + part // 2, place] = rows[first : first + 8].astype(BF16)
 
     def pair_copy(self, part):
         spot = self.spot
@@ -301,34 +305,35 @@
         return send(self.halves.at[other, :, first:end], self.partner.at[:, first:end], self.pair_sems.at[0, part],
                     self.pair_sems.at[1, part], spot.column_peer(spot.x_lo * 2 + other))
 
-    def merge(self, together):
+    def merge_part(self, part):
         core = self.spot.core
-        for part, (first, end) in enumerate(PARTS):
-            self.pair_copy(part).wait_recv()
-            for rank in range(PLANE):
-                own = self.halves[core, rank, first:end].astype(F32)
-                both = own + self.partner[rank, first:end].astype(F32)
-                self.merged[rank, first:end] = both.astype(BF16)
-            if not together:
-                self.plane_start(first, end)
-        if together:
-            self.plane_start(0, DEEP)
-
-    def plane_start(self, first, end):
+        first, end = PARTS[part]
+        self.pair_copy(part).wait_recv()
+        for rank in range(PLANE):
+            own = self.halves[core, rank, first:end].astype(F32)
+            both = own + self.partner[rank, first:end].astype(F32)
+            self.merged[rank, first:end] = both.astype(BF16)
+
+    def merge(self):
+        for part in range(len(PARTS)):
+            self.merge_part(part)
+        self.plane_start(0, 0, DEEP)
+
+    def plane_start(self, part, first, end):
         spot = self.spot
         for x, y in PLANE_STEPS:
             rank, peer = spot.plane_step(x, y)
-            send(self.merged.at[rank, first:end], self.plane_in.at[spot.plane, first:end], self.plane_sems.at[0],
-                 self.plane_sems.at[1], peer).start()
-
-    def plane_whole(self):
-        return send(self.merged.at[0 : PLANE - 1], self.plane_in.at[0 : PLANE - 1], self.plane_sems.at[0],
-                    self.plane_sems.at[1], self.spot.plane_step(1, 0)[1])
+            send(self.merged.at[rank, first:end], self.plane_in.at[spot.plane, first:end], self.plane_sems.at[0, part],
+                 self.plane_sems.at[1, part], peer).start()
+
+    def plane_whole(self, part, first, end):
+        return send(self.merged.at[0 : PLANE - 1, first:end], self.plane_in.at[0 : PLANE - 1, first:end],
+                    self.plane_sems.at[0, part], self.plane_sems.at[1, part], self.spot.plane_step(1, 0)[1])
 
     def plane_finish(self):
         me = self.spot.plane
         self.plane_in[me] = self.merged[me]
-        self.plane_whole().wait_recv()
+        self.plane_whole(0, 0, DEEP).wait_recv()
 
         @pl.loop(0, DEEP)
         def _(z):
@@ -346,9 +351,12 @@
         return send(self.deep_out.at[0 : DEEP - 1], self.deep_in.at[0 : DEEP - 1], self.deep_sems.at[0],
                     self.deep_sems.at[1], self.spot.deep_peer(lax.rem(self.spot.deep + 1, DEEP)))
 
-    def deep_finish(self, out_ref):
+    def keep_own(self):
         me = self.spot.deep
         self.deep_in[me] = self.deep_out[me]
+
+    def deep_finish(self, out_ref):
+        self.keep_own()
         self.deep_whole().wait_recv()
 
         total = jnp.zeros((PIECE, 128), F32)
@@ -367,8 +375,54 @@
     def drain(self):
         for part in range(len(PARTS)):
             self.pair_copy(part).wait_send()
-        self.plane_whole().wait_send()
+        self.drain_plane()
         self.deep_whole().wait_send()
+
+    def drain_plane(self):
+        self.plane_whole(0, 0, DEEP).wait_send()
+
+
+class FarFirst(Scatter):
+    def place(self, z):
+        offset = lax.rem(z - self.spot.deep + DEEP, DEEP)
+        upper = lax.div(offset, 8)
+        return (1 - upper) * (15 - 2 * offset) + upper * (2 * offset - 16)
+
+    def produce(self, cols, delta):
+        for step in range(3):
+            rows = cols[step : step + 8].reshape(512, 9 * 128)
+            self.grad[step * 1152 : (step + 1) * 1152] = lax.dot_general(
+                rows, delta, (((0,), (0,)), ((), ())), preferred_element_type=F32
+            )
+            self.cut(*PARTS[step])
+        for part in range(len(PARTS)):
+            self.pair_copy(part).start()
+
+    def merge(self):
+        for part, (first, end) in enumerate(PARTS):
+            self.merge_part(part)
+            self.plane_start(part, first, end)
+
+    def plane_finish(self):
+        me = self.spot.plane
+        self.plane_in[me] = self.merged[me]
+        for part, (first, end) in enumerate(PARTS):
+            self.plane_whole(part, first, end).wait_recv()
+            total = jnp.zeros((end - first, PIECE, 128), F32)
+            for rank in range(PLANE):
+                total = total + self.plane_in[rank, first:end].astype(F32)
+            self.deep_out[first:end] = total.astype(BF16)
+            for place in range(first, min(end, DEEP - 1)):
+                rank = lax.rem(self.spot.deep + DEEP_STEPS[place], DEEP)
+                send(self.deep_out.at[place], self.deep_in.at[place], self.deep_sems.at[0], self.deep_sems.at[1],
+                     self.spot.deep_peer(rank)).start()
+
+    def keep_own(self):
+        self.deep_in[DEEP - 1] = self.deep_out[DEEP - 1]
+
+    def drain_plane(self):
+        for part, (first, end) in enumerate(PARTS):
+            self.plane_whole(part, first, end).wait_send()
 
 
 def convolve(cols, kernel_ref):
@@ -398,7 +452,7 @@
 
     source_in, upstream_in, back_in = (take(Gather) for _ in range(3))
     halo_one, halo_two, halo_three, halo_four = (take(Halo) for _ in range(4))
-    scatter_one, scatter_two = (take(Scatter) for _ in range(2))
+    scatter_one, scatter_two = take(FarFirst), take(Scatter)
     news = take(News)
     (first_kernel, second_kernel, first_turned, second_turned, centre, lines, source_cols, act_cols, delta_cols, upstream,
      slope_one, slot_tile, slot_used, load_sems) = scratch
@@ -466,12 +520,12 @@
     halo_three.start()
     scatter_two.produce(act_cols, halo_three.tile[...].reshape(512, 128))
     news.hear(2)
+    scatter_two.merge()
     halo_three.finish(centre, lines, masks, delta_cols)
-    scatter_two.merge(together=True)
     halo_four.put(centre, convolve(delta_cols, second_back) * slope_one[...])
     halo_four.start()
     scatter_one.produce(source_cols, halo_four.tile[...].reshape(512, 128))
-    scatter_one.merge(together=False)
+    scatter_one.merge()
     halo_four.finish(centre, lines, masks, delta_cols)
     back_in.tiles[me] = convolve(delta_cols, first_back).astype(BF16)
     back_in.start()

time: 65.9 us -> 62.6 us (0.950)
  Pallas kernels: 64.9 us -> 61.8 us
    pallas_call x1, Pallas kernels: 64.3 us -> 61.2 us  [fused(): pl.pallas_call(body, out_shape=(pltpu.VMEM((512, 128), BF16), piece, piec...]
where the time goes in v5:
time: 62.6 us; the launch traced here: 62.5 us
  Pallas kernels  61.8 us (99%)
  between operations  0.64 us (1%)
    pallas_call x1, Pallas kernels, fused(): pl.pallas_call(body, out_shape=(pltpu.VMEM((512, 128), BF16), piece, piec...  61.2 us

profile of v5, /device:TPU:1, one launch (start us, length us, event | category | flops | bytes accessed | tf_op | source)
XLA Modules:
  0.0 62.5 jit_solution(11742627467581599771)
XLA Ops:
  0.6 61.2 %shard_map.85 = (bf16[512,128]{1,0:T(8,128)(2,1)S(1)}, f32[8,128]{1,0:T(8,128)S(1)}, f32[8,128]{1,0:T(8,128)S(1)}) custom-call(bf16[512,128]{1,0:T(8,128)(2,1)} %bitcast.3, bf16[512,128]{1,0:T(8,128)(2,1)} %bitcast.4, bf16[27,128,128]{2,1,0:T(8,128)(2,1)} %first_hbm.1, bf16[27,128,128]{2,1,0:T(8,128)(2,1)} %second_hbm.1, s32[1,4]{1,0:T(1,128)} %tile_hbm.1, ...), custom_call_target="tpu_custom_call" | custom-call | tf_op jit(solution)/shard_map/pallas_call | solution.py:566
  61.8 0.7 %shard_map.86 = (bf16[512,128]{1,0:T(8,128)(2,1)}, f32[864]{0:T(1024)}, f32[864]{0:T(1024)}) custom-call(bf16[512,128]{1,0:T(8,128)(2,1)S(1)} %get-tuple-element.9.grad, f32[8,128]{1,0:T(8,128)S(1)} %get-tuple-element.10.first, f32[8,128]{1,0:T(8,128)S(1)} %get-tuple-element.11.second), custom_call_target="tpu_custom_call" | custom-call | tf_op jit(solution)/shard_map/pallas_call | solution.py:582

commit v6 on v5

--- a/solution.py
+++ b/solution.py
@@ -21,6 +21,7 @@
 )
 DEEP_STEPS = (8, 7, 9, 6, 10, 5, 11, 4, 12, 3, 13, 2, 14, 1, 15)
 PARTS = ((0, 5), (5, 10), (10, DEEP))
+FAR_PARTS = ((0, 2), (2, 5), (5, 9), (9, DEEP))
 F32 = jnp.float32
 BF16 = jnp.bfloat16
 
@@ -116,14 +117,18 @@
     def scratch():
         return [pltpu.VMEM((4, 512, 128), BF16), pltpu.SemaphoreType.DMA((2, 4))]
 
-    def part(self, tile, half, way, peer):
+    def part(self, tile, half, way, peer, source=None):
         rows = self.tiles.at[tile] if half is None else self.tiles.at[tile, half * 256 : (half + 1) * 256]
-        return send(rows, rows, self.sems.at[0, way], self.sems.at[1, way], self.spot.column_peer(peer))
-
-    def start(self):
+        if source is None:
+            own = rows
+        else:
+            own = source if half is None else source.at[half * 256 : (half + 1) * 256]
+        return send(own, rows, self.sems.at[0, way], self.sems.at[1, way], self.spot.column_peer(peer))
+
+    def start(self, source=None):
         for half in range(2):
-            self.part(self.me, half, half, self.across).start()
-        self.part(self.me, None, 2, self.pair).start()
+            self.part(self.me, half, half, self.across, source).start()
+        self.part(self.me, None, 2, self.pair, source).start()
 
     def relay(self):
         for half in range(2):
@@ -254,6 +259,8 @@
 
 
 class Scatter:
+    parts = PARTS
+
     def __init__(self, spot, refs):
         self.spot = spot
         (self.halves, self.partner, self.merged, self.plane_in, self.deep_out, self.deep_in, self.grad, self.pair_sems,
@@ -269,8 +276,8 @@
             pltpu.VMEM((DEEP, PIECE, 128), BF16),
             pltpu.VMEM((DEEP, PIECE, 128), BF16),
             pltpu.VMEM((ROWS, 128), F32),
-            pltpu.SemaphoreType.DMA((2, len(PARTS))),
-            pltpu.SemaphoreType.DMA((2, len(PARTS))),
+            pltpu.SemaphoreType.DMA((2, 4)),
+            pltpu.SemaphoreType.DMA((2, 4)),
             pltpu.SemaphoreType.DMA((2,)),
         ]
 
@@ -301,13 +308,13 @@
     def pair_copy(self, part):
         spot = self.spot
         other = 1 - spot.core
-        first, end = PARTS[part]
+        first, end = self.parts[part]
         return send(self.halves.at[other, :, first:end], self.partner.at[:, first:end], self.pair_sems.at[0, part],
                     self.pair_sems.at[1, part], spot.column_peer(spot.x_lo * 2 + other))
 
     def merge_part(self, part):
         core = self.spot.core
-        first, end = PARTS[part]
+        first, end = self.parts[part]
         self.pair_copy(part).wait_recv()
         for rank in range(PLANE):
             own = self.halves[core, rank, first:end].astype(F32)
@@ -315,7 +322,7 @@
             self.merged[rank, first:end] = both.astype(BF16)
 
     def merge(self):
-        for part in range(len(PARTS)):
+        for part in range(len(self.parts)):
             self.merge_part(part)
         self.plane_start(0, 0, DEEP)
 
@@ -373,7 +380,7 @@
         out_ref[...] = share
 
     def drain(self):
-        for part in range(len(PARTS)):
+        for part in range(len(self.parts)):
             self.pair_copy(part).wait_send()
         self.drain_plane()
         self.deep_whole().wait_send()
@@ -383,6 +390,8 @@
 
 
 class FarFirst(Scatter):
+    parts = FAR_PARTS
+
     def place(self, z):
         offset = lax.rem(z - self.spot.deep + DEEP, DEEP)
         upper = lax.div(offset, 8)
@@ -395,18 +404,18 @@
                 rows, delta, (((0,), (0,)), ((), ())), preferred_element_type=F32
             )
             self.cut(*PARTS[step])
-        for part in range(len(PARTS)):
+        for part in range(len(self.parts)):
             self.pair_copy(part).start()
 
     def merge(self):
-        for part, (first, end) in enumerate(PARTS):
+        for part, (first, end) in enumerate(self.parts):
             self.merge_part(part)
             self.plane_start(part, first, end)
 
     def plane_finish(self):
         me = self.spot.plane
         self.plane_in[me] = self.merged[me]
-        for part, (first, end) in enumerate(PARTS):
+        for part, (first, end) in enumerate(self.parts):
             self.plane_whole(part, first, end).wait_recv()
             total = jnp.zeros((end - first, PIECE, 128), F32)
             for rank in range(PLANE):
@@ -421,7 +430,7 @@
         self.deep_in[DEEP - 1] = self.deep_out[DEEP - 1]
 
     def drain_plane(self):
-        for part, (first, end) in enumerate(PARTS):
+        for part, (first, end) in enumerate(self.parts):
             self.plane_whole(part, first, end).wait_send()
 
 
@@ -469,10 +478,9 @@
     for load in loads:
         load.start()
     greet(spot)
-    loads[0].wait()
-    source_in.start()
+    source_in.start(features)
     news.tell(0)
-    for load in loads[1:3]:
+    for load in loads[:3]:
         load.wait()
 
     weights = [jnp.where(slot_tile[0, j] == me, 1.0, 0.0) * slot_used[0, j].astype(F32) for j in range(4)]
@@ -499,7 +507,7 @@
     halo_one.start()
     for load in loads[3:]:
         load.wait()
-    upstream_in.start()
+    upstream_in.start(cotangent)
     turn(first_kernel, first_turned)
     news.hear(0)
     news.tell(1)

time: 62.6 us -> 62.9 us (level)
  no operation moved by 1% of the time
where the time goes in v6:
time: 62.9 us; the launch traced here: 62.7 us
  Pallas kernels  62.1 us (99%)
  between operations  0.64 us (1%)
    pallas_call x1, Pallas kernels, fused(): pl.pallas_call(body, out_shape=(pltpu.VMEM((512, 128), BF16), piece, piec...  61.4 us

profile of v6, /device:TPU:1, one launch (start us, length us, event | category | flops | bytes accessed | tf_op | source)
XLA Modules:
  0.0 62.7 jit_solution(4176090834352845147)
XLA Ops:
  0.6 61.4 %shard_map.85 = (bf16[512,128]{1,0:T(8,128)(2,1)S(1)}, f32[8,128]{1,0:T(8,128)S(1)}, f32[8,128]{1,0:T(8,128)S(1)}) custom-call(bf16[512,128]{1,0:T(8,128)(2,1)} %bitcast.3, bf16[512,128]{1,0:T(8,128)(2,1)} %bitcast.4, bf16[27,128,128]{2,1,0:T(8,128)(2,1)} %first_hbm.1, bf16[27,128,128]{2,1,0:T(8,128)(2,1)} %second_hbm.1, s32[1,4]{1,0:T(1,128)} %tile_hbm.1, ...), custom_call_target="tpu_custom_call" | custom-call | tf_op jit(solution)/shard_map/pallas_call | solution.py:574
  62.1 0.7 %shard_map.86 = (bf16[512,128]{1,0:T(8,128)(2,1)}, f32[864]{0:T(1024)}, f32[864]{0:T(1024)}) custom-call(bf16[512,128]{1,0:T(8,128)(2,1)S(1)} %get-tuple-element.9.grad, f32[8,128]{1,0:T(8,128)S(1)} %get-tuple-element.10.first, f32[8,128]{1,0:T(8,128)S(1)} %get-tuple-element.11.second), custom_call_target="tpu_custom_call" | custom-call | tf_op jit(solution)/shard_map/pallas_call | solution.py:590

commit v7 on v5

--- a/solution.py
+++ b/solution.py
@@ -268,7 +268,7 @@
             pltpu.VMEM((PLANE, DEEP, PIECE, 128), BF16),
             pltpu.VMEM((DEEP, PIECE, 128), BF16),
             pltpu.VMEM((DEEP, PIECE, 128), BF16),
-            pltpu.VMEM((ROWS, 128), F32),
+            pltpu.VMEM((ROWS + 8, 128), F32),
             pltpu.SemaphoreType.DMA((2, len(PARTS))),
             pltpu.SemaphoreType.DMA((2, len(PARTS))),
             pltpu.SemaphoreType.DMA((2,)),
@@ -291,12 +291,10 @@
         @pl.loop(first_z, end_z)
         def _(z):
             place = self.place(z)
-            rows = self.grad[pl.ds(pl.multiple_of(z * 216, 8), 216), :]
-            rows = jnp.concatenate([rows, jnp.zeros((8, 128), F32)], axis=0)
             for column in range(8):
                 for part in range(4):
                     first = column * 27 + part * 27 // 4
-                    self.halves[part % 2, column * 2 + part // 2, place] = rows[first : first + 8].astype(BF16)
+                    self.halves[part % 2, column * 2 + part // 2, place] = self.grad[pl.ds(z * 216 + first, 8), :].astype(BF16)
 
     def pair_copy(self, part):
         spot = self.spot
@@ -501,6 +499,8 @@
         load.wait()
     upstream_in.start()
     turn(first_kernel, first_turned)
+    for scatter in (scatter_one, scatter_two):
+        scatter.grad[ROWS : ROWS + 8] = jnp.zeros((8, 128), F32)
     news.hear(0)
     news.tell(1)
     halo_one.finish(centre, lines, masks, source_cols)

time: 62.6 us -> 62.3 us (level)
  no operation moved by 1% of the time
where the time goes in v7:
time: 62.3 us; the launch traced here: 62.2 us
  Pallas kernels  61.5 us (99%)
  between operations  0.64 us (1%)
    pallas_call x1, Pallas kernels, fused(): pl.pallas_call(body, out_shape=(pltpu.VMEM((512, 128), BF16), piece, piec...  60.9 us

profile of v7, /device:TPU:1, one launch (start us, length us, event | category | flops | bytes accessed | tf_op | source)
XLA Modules:
  0.0 62.2 jit_solution(18416016802712079658)
XLA Ops:
  0.6 60.9 %shard_map.85 = (bf16[512,128]{1,0:T(8,128)(2,1)S(1)}, f32[8,128]{1,0:T(8,128)S(1)}, f32[8,128]{1,0:T(8,128)S(1)}) custom-call(bf16[512,128]{1,0:T(8,128)(2,1)} %bitcast.3, bf16[512,128]{1,0:T(8,128)(2,1)} %bitcast.4, bf16[27,128,128]{2,1,0:T(8,128)(2,1)} %first_hbm.1, bf16[27,128,128]{2,1,0:T(8,128)(2,1)} %second_hbm.1, s32[1,4]{1,0:T(1,128)} %tile_hbm.1, ...), custom_call_target="tpu_custom_call" | custom-call | tf_op jit(solution)/shard_map/pallas_call | solution.py:566
  61.5 0.7 %shard_map.86 = (bf16[512,128]{1,0:T(8,128)(2,1)}, f32[864]{0:T(1024)}, f32[864]{0:T(1024)}) custom-call(bf16[512,128]{1,0:T(8,128)(2,1)S(1)} %get-tuple-element.9.grad, f32[8,128]{1,0:T(8,128)S(1)} %get-tuple-element.10.first, f32[8,128]{1,0:T(8,128)S(1)} %get-tuple-element.11.second), custom_call_target="tpu_custom_call" | custom-call | tf_op jit(solution)/shard_map/pallas_call | solution.py:582
